TPU v7x, 32 devices: a whole 2x2x4 slice. The times are simulated.
32 devices in a mesh: band: 4 (over z), sector: 8 (over y, x, core).
Axes of the slice: x: 2, y: 2, z: 4, core: 2. Of those that a mesh axis runs over, the one named last changes fastest.
Arguments:
- node_states: bfloat16 [16, 128, 512], P('band', 'sector'), may hold values from -6 to 6
- edge_states: bfloat16 [32, 512, 512], P(('band', 'sector')), may hold values from -6 to 6
- senders: int32 [32, 512], P(('band', 'sector')), may hold values from 0 to 351, as said below
- receivers: int32 [32, 512], P(('band', 'sector')), may hold values from 0 to 63
- edge_count: int32 [32], P(('band', 'sector')), may hold values from 128 to 512, as said below
- edge_hidden: bfloat16 [2, 1536, 512], replicated, may hold values from -0.15625 to 0.15625
- edge_offset: float32 [2, 512], replicated, may hold values from -3 to 3
- edge_output: bfloat16 [2, 512, 512], replicated, may hold values from -0.25 to 0.25
- edge_scale: float32 [2, 512], replicated, may hold values from 0.5 to 1.5
- node_hidden: bfloat16 [2, 1024, 512], replicated, may hold values from -0.1875 to 0.1875
- node_offset: float32 [2, 512], replicated, may hold values from -3 to 3
- node_output: bfloat16 [2, 512, 512], replicated, may hold values from -0.25 to 0.25
- node_scale: float32 [2, 512], replicated, may hold values from 0.5 to 1.5
- output_cotangent: bfloat16 [16, 128, 512], P('band', 'sector'), may hold values from -6 to 6
Outputs:
- node_result: bfloat16 [16, 128, 512], P('band', 'sector')
- node_gradient: float32 [16, 128, 512], P('band', 'sector')
- edge_gradient: float32 [32, 512, 512], P(('band', 'sector'))
- edge_hidden_gradient: float32 [2, 1536, 512], replicated
- edge_offset_gradient: float32 [2, 512], replicated
- edge_output_gradient: float32 [2, 512, 512], replicated
- edge_scale_gradient: float32 [2, 512], replicated
- node_hidden_gradient: float32 [2, 1024, 512], replicated
- node_offset_gradient: float32 [2, 512], replicated
- node_output_gradient: float32 [2, 512, 512], replicated
- node_scale_gradient: float32 [2, 512], replicated
Inputs may be any that keep to these rules, and one draw needn't show every extreme that they name: `senders`: an entry below 288 names a cell of the device's extended block (row-major, 12 rows); devices of the first band never name its first 4 rows, devices of the last band never its last 4 rows. An entry 288 + c names coarse node c. `edge_count`: slots at or past a device's count hold no edge. Some device has all 512 slots live.
All inputs are finite; a program needn't handle non-finite values.
Results may differ from a plain program's by a relative error of at most 0.019.
Values may be sent and summed in bfloat16 or wider, within the bound.
No kernel may reach another device: no remote copies, remote signals or barrier semaphores. Data moves between devices by JAX's collectives and lax.ppermute only.
A program may use at most 128 MiB of HBM per device.

v0:
```python
import math

import jax
import jax.numpy as jnp
from jax import lax
from jax.sharding import PartitionSpec as P

CO = 2


epsilon = 1e-05


def shifted(shard, axis, by):
    length = lax.axis_size(axis)
    return lax.ppermute(shard, axis, [(i, (i + by) % length) for i in range(length)])


def passed_along(block, axis, distance):
    devices = range(lax.axis_size(axis))
    route = [(i - distance, i) for i in devices if i - distance in devices]
    return lax.ppermute(block, axis, route)


def extended_2(cells, sides, width):
    for axis, dim in sides:
        count = lax.axis_size(axis)
        head = lax.slice_in_dim(cells, 0, width, axis=dim)
        tail = lax.slice_in_dim(cells, cells.shape[dim] - width, cells.shape[dim], axis=dim)
        cells = jnp.concatenate(
            [
                lax.ppermute(tail, axis, [(i, (i + 1) % count) for i in range(count)]),
                cells,
                lax.ppermute(head, axis, [((i + 1) % count, i) for i in range(count)]),
            ],
            axis=dim,
        )
    return cells


def mlp_forward(inputs, first_weight, first_bias, second_weight, norm_gain):
    pre_act = jnp.dot(inputs, first_weight, preferred_element_type=jnp.float32) + first_bias
    sigmoid_val = jax.nn.sigmoid(pre_act)
    activated = (pre_act * sigmoid_val).astype(jnp.bfloat16)
    mixed = jnp.dot(activated, second_weight, preferred_element_type=jnp.float32)
    centered = mixed - jnp.mean(mixed, axis=-1, keepdims=True)
    inv_std = lax.rsqrt(jnp.mean(centered * centered, axis=-1, keepdims=True) + epsilon)
    normed = centered * inv_std
    return (normed * norm_gain, (inputs, pre_act, sigmoid_val, activated, normed, inv_std))


def mlp_backward(grad_out, saved, first_weight, second_weight, norm_gain):
    inputs, pre_act, sigmoid_val, activated, normed, inv_std = saved
    grad_gain = jnp.sum(grad_out * normed, axis=0)
    grad_normed = grad_out * norm_gain
    grad_mixed = inv_std * (
        grad_normed
        - jnp.mean(grad_normed, axis=-1, keepdims=True)
        - normed * jnp.mean(grad_normed * normed, axis=-1, keepdims=True)
    )
    mixed_low = grad_mixed.astype(jnp.bfloat16)
    grad_second = lax.dot_general(
        activated, mixed_low, (((0,), (0,)), ((), ())), preferred_element_type=jnp.float32
    )
    grad_act = lax.dot_general(
        mixed_low, second_weight, (((1,), (1,)), ((), ())), preferred_element_type=jnp.float32
    )
    grad_pre = grad_act * sigmoid_val * (1.0 + pre_act * (1.0 - sigmoid_val))
    grad_bias = jnp.sum(grad_pre, axis=0)
    pre_low = grad_pre.astype(jnp.bfloat16)
    grad_first = lax.dot_general(
        inputs, pre_low, (((0,), (0,)), ((), ())), preferred_element_type=jnp.float32
    )
    grad_inputs = lax.dot_general(
        pre_low, first_weight, (((1,), (1,)), ((), ())), preferred_element_type=jnp.float32
    )
    return (grad_inputs, (grad_first, grad_bias, grad_second, grad_gain))


def fold_sector(grad_block, reach):
    kept = grad_block.shape[1] - 2 * reach
    middle = grad_block[:, reach : reach + kept]
    from_next = shifted(grad_block[:, :reach].astype(jnp.bfloat16), "sector", -1).astype(
        jnp.float32
    )
    from_prev = shifted(grad_block[:, reach + kept :].astype(jnp.bfloat16), "sector", 1).astype(
        jnp.float32
    )
    return middle.at[:, kept - reach :].add(from_next).at[:, :reach].add(from_prev)


def fold_band(grad_block, reach):
    kept = grad_block.shape[0] - 2 * reach
    middle = grad_block[reach : reach + kept]
    from_next = passed_along(grad_block[:reach].astype(jnp.bfloat16), "band", -1).astype(
        jnp.float32
    )
    from_prev = passed_along(grad_block[reach + kept :].astype(jnp.bfloat16), "band", 1).astype(
        jnp.float32
    )
    return middle.at[kept - reach :].add(from_next).at[:reach].add(from_prev)


def local(
    node_states,
    edge_states,
    senders,
    receivers,
    edge_count,
    edge_hidden,
    edge_offset,
    edge_output,
    edge_scale,
    node_hidden,
    node_offset,
    node_output,
    node_scale,
    output_cotangent,
):
    lat_rows, lon_cols, width = node_states.shape
    node_rows = lat_rows * lon_cols
    slots = edge_states.shape[1]
    depth = edge_hidden.shape[0]
    ext_rows = 3 * lat_rows * (lon_cols + 2 * lat_rows)
    table_rows = ext_rows + CO * lax.axis_size("band") * lax.axis_size("sector")
    edge_rows = edge_states[0]
    send_index = senders[0]
    recv_index = receivers[0]
    live_count = edge_count[0]
    live_mask = (jnp.arange(slots, dtype=jnp.int32) < live_count).astype(jnp.float32)[:, None]
    incidence = (recv_index[:, None] == jnp.arange(node_rows, dtype=jnp.int32)[None, :]).astype(
        jnp.float32
    )
    sender_onehot = (
        send_index[:, None] == jnp.arange(table_rows, dtype=jnp.int32)[None, :]
    ).astype(jnp.float32)
    state = node_states.reshape(node_rows, width)
    records = []
    for depth_index in range(depth):
        edge_params = (
            edge_hidden[depth_index],
            edge_offset[depth_index],
            edge_output[depth_index],
            edge_scale[depth_index],
        )
        node_params = (
            node_hidden[depth_index],
            node_offset[depth_index],
            node_output[depth_index],
            node_scale[depth_index],
        )
        extended = extended_2(
            state.reshape(lat_rows, lon_cols, width), (("band", 0), ("sector", 1)), lat_rows
        )
        coarse = lax.all_gather(state[:CO], ("band", "sector"), axis=0, tiled=True)
        table = jnp.concatenate([extended.reshape(ext_rows, width), coarse], axis=0)
        inputs = jnp.concatenate(
            [edge_rows, jnp.take(table, send_index, axis=0), jnp.take(state, recv_index, axis=0)],
            axis=1,
        )
        result, edge_saved = mlp_forward(
            inputs, edge_params[0], edge_params[1], edge_params[2], edge_params[3]
        )
        update = result * live_mask
        summed = lax.dot_general(
            incidence,
            update,
            (((0,), (0,)), ((), ())),
            precision=lax.Precision.HIGHEST,
            preferred_element_type=jnp.float32,
        )
        node_inputs = jnp.concatenate([state, summed.astype(jnp.bfloat16)], axis=1)
        node_delta, node_saved = mlp_forward(
            node_inputs, node_params[0], node_params[1], node_params[2], node_params[3]
        )
        records.append((inputs, edge_saved, node_saved))
        edge_rows = (edge_rows.astype(jnp.float32) + update).astype(jnp.bfloat16)
        state = (state.astype(jnp.float32) + node_delta).astype(jnp.bfloat16)
    node_result = state.reshape(lat_rows, lon_cols, width)
    grad_state = output_cotangent.reshape(node_rows, width).astype(jnp.float32)
    grad_edges = jnp.zeros((slots, width), jnp.float32)
    per_layer = [None] * depth
    for depth_index in reversed(range(depth)):
        inputs, edge_saved, node_saved = records[depth_index]
        edge_params = (
            edge_hidden[depth_index],
            edge_offset[depth_index],
            edge_output[depth_index],
            edge_scale[depth_index],
        )
        grad_in, node_grads = mlp_backward(
            grad_state,
            node_saved,
            node_hidden[depth_index],
            node_output[depth_index],
            node_scale[depth_index],
        )
        grad_state = grad_state + grad_in[:, :width]
        spread = jnp.dot(
            incidence,
            grad_in[:, width:],
            precision=lax.Precision.HIGHEST,
            preferred_element_type=jnp.float32,
        )
        flow_grad = (spread + grad_edges) * live_mask
        grad_inputs, edge_grads = mlp_backward(
            flow_grad, edge_saved, edge_params[0], edge_params[2], edge_params[3]
        )
        grad_edges = grad_edges + grad_inputs[:, :width]
        grad_state = grad_state + lax.dot_general(
            incidence,
            grad_inputs[:, 2 * width :],
            (((0,), (0,)), ((), ())),
            precision=lax.Precision.HIGHEST,
            preferred_element_type=jnp.float32,
        )
        table_grad = lax.dot_general(
            sender_onehot,
            grad_inputs[:, width : 2 * width],
            (((0,), (0,)), ((), ())),
            precision=lax.Precision.HIGHEST,
            preferred_element_type=jnp.float32,
        )
        ext_grad = table_grad[:ext_rows].reshape(3 * lat_rows, lon_cols + 2 * lat_rows, width)
        coarse_grad = table_grad[ext_rows:]
        returned = fold_band(fold_sector(ext_grad, lat_rows), lat_rows)
        grad_state = grad_state + returned.reshape(node_rows, width)
        layer_grads = edge_grads + node_grads
        summed_grads = lax.psum(
            (
                layer_grads[0],
                layer_grads[1],
                layer_grads[2],
                layer_grads[3],
                layer_grads[4],
                layer_grads[5],
                layer_grads[6],
                layer_grads[7],
                coarse_grad,
            ),
            ("band", "sector"),
        )
        own_coarse = lax.dynamic_slice_in_dim(
            summed_grads[8], lax.axis_index(("band", "sector")) * CO, CO, 0
        )
        per_layer[depth_index] = tuple(summed_grads[:8])
        grad_state = grad_state.at[:CO].add(own_coarse)
    stacked = [
        jnp.stack([per_layer[depth_index][item] for depth_index in range(depth)])
        for item in range(8)
    ]
    factor = 1.0 / math.sqrt(node_rows * lax.axis_size("band") * lax.axis_size("sector"))
    return (
        node_result,
        grad_state.reshape(lat_rows, lon_cols, width),
        grad_edges[None],
        stacked[0] * factor,
        stacked[1] * factor,
        stacked[2] * factor,
        stacked[3] * factor,
        stacked[4] * factor,
        stacked[5] * factor,
        stacked[6] * factor,
        stacked[7] * factor,
    )


def solution(mesh):
    return jax.shard_map(
        local,
        mesh=mesh,
        in_specs=(
            P("band", "sector", None),
            P(("band", "sector"), None, None),
            P(("band", "sector"), None),
            P(("band", "sector"), None),
            P(("band", "sector")),
            P(),
            P(),
            P(),
            P(),
            P(),
            P(),
            P(),
            P(),
            P("band", "sector", None),
        ),
        out_specs=(
            P("band", "sector", None),
            P("band", "sector", None),
            P(("band", "sector"), None, None),
            P(),
            P(),
            P(),
            P(),
            P(),
            P(),
            P(),
            P(),
        ),
        check_vma=False,
    )
```

profile of v0, /device:TPU:0, one launch (start us, length us, event | category | flops | bytes accessed | tf_op | source)
XLA Modules:
  0.0 573.9 jit_solution(11229786818335599624)
XLA Ops:
  7.3 3.1 collective-permute-start
  10.4 2.1 collective-permute-start.1
  15.3 2.9 gather_fusion.1
  20.6 1.7 collective-permute-start.3
  22.3 39.2 %all-gather = bf16[32,2,512]{2,1,0:T(2,128)(2,1)S(1)} all-gather(bf16[1,2,512]{2,1,0:T(2,128)(2,1)S(1)} %slice_bitcast_fusion.1), channel_id=1, replica_groups=mesh['band'=4,'sector'=8] {'band','sector'}, dimensions={0}, use_global_device_ids=true | all-gather | bytes 67584 | tf_op jit(solution)/shard_map/all_gather | solution.py:155
  62.5 2.0 gather_fusion
  64.8 2.6 fusion.15
  70.5 2.0 gather_fusion.3
  72.6 2.0 collective-permute-start.4
  76.9 1.9 collective-permute-done.4
  79.4 37.3 %all-gather.1 = bf16[32,2,512]{2,1,0:T(2,128)(2,1)S(1)} all-gather(bf16[1,2,512]{2,1,0:T(2,128)(2,1)S(1)} %slice_bitcast_fusion), channel_id=1, replica_groups=mesh['band'=4,'sector'=8] {'band','sector'}, dimensions={0}, use_global_device_ids=true | all-gather | bytes 67584 | tf_op jit(solution)/shard_map/all_gather | solution.py:155
  117.0 2.0 gather_fusion.2
  119.2 2.7 fusion.18
  128.0 1.6 multiply_reduce_fusion
  130.0 1.3 fusion.125
  132.9 2.7 convolution_bitcast_fusion
  135.6 1.5 convolution_bitcast_fusion.6
  138.9 1.3 convolution_bitcast_fusion.4
  142.0 1.6 copy.41
  145.1 3.2 collective-permute-done.9
  149.2 1.3 collective-permute-start.11
  150.5 1.5 collective-permute-start.10
  152.0 1.8 convolution_bitcast_fusion.2
  153.8 2.9 collective-permute-done.10
  156.7 1.8 bitcast_add_fusion.1
  158.5 109.4 %all-reduce.5.cloned.1.call-done = f32[64,512]{1,0:T(8,128)} async-done(((f32[64,512]{1,0:T(8,128)}), f32[64,512]{1,0:T(8,128)}) %all-reduce.5.cloned.1.call-update) | async-done | bytes 131088 | tf_op jit(solution)/shard_map/psum | solution.py:229
  269.6 1.4 fusion.128
  271.0 1.7 fusion.32
  277.2 2.7 convolution_bitcast_fusion.1
  279.9 1.5 convolution_bitcast_fusion.7
  281.4 1.8 convolution_bitcast_fusion.3
  283.2 1.4 convolution_bitcast_fusion.5
  290.1 2.5 copy.42
  292.6 42.0 %all-reduce = (f32[1,512]{1,0:T(1,128)S(1)}, f32[1,512]{1,0:T(1,128)S(1)}, f32[1,512]{1,0:T(1,128)S(1)}, f32[1,512]{1,0:T(1,128)S(1)}, f32[1,512]{1,0:T(1,128)S(...) all-reduce(f32[1,512]{1,0:T(1,128)S(1)} %bitcast.197, ...), channel_id=1, replica_groups=mesh['band'=4,'sector'=8] {'band','sector'}, use_global_device_ids=true, to_apply=%region_23.26 | all-reduce | flops 4096 | bytes 32768 | tf_op jit(solution)/shard_map/psum | solution.py:229
  335.8 2.8 add_bitcast_fusion
  340.1 2.5 copy.40
  342.6 1.6 fusion.94
  344.2 1.6 fusion.93
  346.9 2.5 collective-permute-start.15
  349.4 1.3 collective-permute-start.14
  351.3 1.6 collective-permute-done.15
  353.0 4.3 collective-permute-done.14
  358.2 1.5 bitcast_add_fusion
  359.7 193.0 %all-reduce.7.cloned.1.call-done = (f32[64,512]{1,0:T(8,128)}, f32[1,1536,512]{2,1,0:T(8,128)}, f32[1,1536,512]{2,1,0:T(8,128)}, f32[1,512,512]{2,1,0:T(8,128)},...) async-done(((f32[64,512]{1,0:T(8,128)}, f32[1,1536,512]{2,1,0:T(8,128)}, ...) | async-done | bytes 14811152 | tf_op jit(solution)/shard_map/psum | solution.py:229
  553.5 6.5 %maximum_multiply_fusion = f32[2,1536,512]{2,1,0:T(8,128)} fusion(f32[1,1536,512]{2,1,0:T(8,128)} %get-tuple-element.207, f32[1,1536,512]{2,1,0:T(8,128)} %get-tuple-element.208), kind=kLoop, calls=%fused_computation.4 | loop fusion | flops 3145728 | bytes 12582912 | tf_op jit(solution)/shard_map/mul | solution.py:257
  560.0 1.6 maximum_multiply_fusion.2
  563.0 2.5 maximum_multiply_fusion.1
  565.5 1.6 maximum_multiply_fusion.3
  (256 shorter events, 45.0 us)
Async XLA Ops:
  7.2 11.2 %copy-start.49 = (f32[2,512]{1,0:T(2,128)S(1)}, f32[2,512]{1,0:T(2,128)}, u32[]{:S(2)}) copy-start(f32[2,512]{1,0:T(2,128)} %param.52) | copy-start | bytes 12292
  7.2 11.9 %copy-start.50 = (f32[2,512]{1,0:T(2,128)S(1)}, f32[2,512]{1,0:T(2,128)}, u32[]{:S(2)}) copy-start(f32[2,512]{1,0:T(2,128)} %param.54) | copy-start | bytes 12292
  7.2 12.5 %copy-start.51 = (f32[2,512]{1,0:T(2,128)S(1)}, f32[2,512]{1,0:T(2,128)}, u32[]{:S(2)}) copy-start(f32[2,512]{1,0:T(2,128)} %param.56) | copy-start | bytes 12292
  7.2 13.0 %copy-start.52 = (f32[2,512]{1,0:T(2,128)S(1)}, f32[2,512]{1,0:T(2,128)}, u32[]{:S(2)}) copy-start(f32[2,512]{1,0:T(2,128)} %param.58) | copy-start | bytes 12292
  7.2 13.0 %copy-start.14 = (bf16[4,16,512]{2,1,0:T(8,128)(2,1)S(1)}, bf16[4,16,512]{2,1,0:T(8,128)(2,1)}, u32[]{:S(2)}) copy-start(bf16[4,16,512]{2,1,0:T(8,128)(2,1)} %param.59) | copy-start | bytes 196612
  7.2 260.8 %all-reduce.5.cloned.1.call-start = ((), (), s32[]{:S(2)}) async-start(), calls=%async_computation | async-start | bytes 262144 | tf_op jit(solution)/shard_map/psum | solution.py:229
  7.3 13.2 %collective-permute-start = (bf16[4,16,512]{2,1,0:T(8,128)(2,1)}, bf16[4,16,512]{2,1,0:T(8,128)(2,1)S(1)}, u32[]{:S(2)}, u32[]{:S(2)}) collective-permute-start(bf16[4,16,512]{2,1,0:T(8,128)(2,1)} %param.46), channel_id=1, source_target_pairs={{0,8},{8,16},{16,24},{24,0},{1,9},{9,17},{17,25},{25,1},{2,10},{10... | collective-permute-start | bytes 196616 | tf_op jit(solution)/shard_map/ppermute | solution.py:32
  10.4 10.1 %collective-permute-start.1 = (bf16[4,16,512]{2,1,0:T(8,128)(2,1)}, bf16[4,16,512]{2,1,0:T(8,128)(2,1)S(1)}, u32[]{:S(2)}, u32[]{:S(2)}) collective-permute-start(bf16[4,16,512]{2,1,0:T(8,128)(2,1)} %param.46), channel_id=1, source_target_pairs={{8,0},{16,8},{24,16},{0,24},{9,1},{17,9},{25,17},{1,25},{10,2},{18... | collective-permute-start | bytes 196616 | tf_op jit(solution)/shard_map/ppermute | solution.py:34
  15.3 5.2 copy-start
  15.3 46.2 %copy-start.22 = (bf16[1,512,512]{2,1,0:T(8,128)(2,1)S(1)}, bf16[1,512,512]{2,1,0:T(8,128)(2,1)}, u32[]{:S(2)}) copy-start(bf16[1,512,512]{2,1,0:T(8,128)(2,1)} %param.47) | copy-start | bytes 1572868
  19.7 54.9 %copy-start.35 = (f32[1,512]{1,0:T(1,128)}, f32[1,512]{1,0:T(1,128)S(1)}, u32[]{:S(2)}) copy-start(f32[1,512]{1,0:T(1,128)S(1)} %get-tuple-element.234) | copy-start | bytes 6148
  20.4 44.4 %copy-start.23 = (bf16[512,512]{0,1:T(8,128)(2,1)}, bf16[512,512]{0,1:T(8,128)(2,1)S(1)}, u32[]{:S(2)}) copy-start(bf16[512,512]{0,1:T(8,128)(2,1)S(1)} %broadcast_select_fusion.1) | copy-start | bytes 1572868
  20.6 41.8 %collective-permute-start.3 = (bf16[12,4,512]{2,1,0:T(4,128)(2,1)S(1)}, bf16[12,4,512]{2,1,0:T(4,128)(2,1)S(1)}, u32[]{:S(2)}, u32[]{:S(2)}) collective-permute-start(bf16[12,4,512]{2,1,0:T(4,128)(2,1)S(1)} %get-tuple-element.226), channel_id=1, source_target_pairs={{1,0},{2,1},{3,2},{4,3},{5,4},{6,5},{7,6},{0,7},{9,8},{10,9},{11,1... | collective-permute-start | bytes 147464 | tf_op jit(solution)/shard_map/ppermute | solution.py:34
  22.2 40.1 %collective-permute-start.2 = (bf16[12,4,512]{2,1,0:T(4,128)(2,1)S(1)}, bf16[12,4,512]{2,1,0:T(4,128)(2,1)S(1)}, u32[]{:S(2)}, u32[]{:S(2)}) collective-permute-start(bf16[12,4,512]{2,1,0:T(4,128)(2,1)S(1)} %get-tuple-element.225), channel_id=1, source_target_pairs={{0,1},{1,2},{2,3},{3,4},{4,5},{5,6},{6,7},{7,0},{8,9},{9,10},{10,1... | collective-permute-start | bytes 147464 | tf_op jit(solution)/shard_map/ppermute | solution.py:32
  22.2 52.4 %copy-start.40 = (f32[512]{0:T(512)}, f32[512]{0:T(512)S(1)}, u32[]{:S(2)}) copy-start(f32[512]{0:T(512)S(1)} %fusion.103) | copy-start | bytes 6148
  61.7 12.9 %copy-start.10 = (bf16[1,512,512]{1,2,0:T(8,128)(2,1)}, bf16[1,512,512]{1,2,0:T(8,128)(2,1)S(1)}, u32[]{:S(2)}) copy-start(bf16[1,512,512]{1,2,0:T(8,128)(2,1)S(1)} %copy.33) | copy-start | bytes 1572868
  68.4 6.2 %copy-start.37 = (f32[512]{0:T(512)}, f32[512]{0:T(512)S(1)}, u32[]{:S(2)}) copy-start(f32[512]{0:T(512)S(1)} %add_rsqrt_fusion.1) | copy-start | bytes 6148
  70.1 5.6 copy-start.43
  70.3 5.4 copy-start.47
  72.5 4.4 collective-permute-start.5
  72.6 6.2 %collective-permute-start.4 = (bf16[4,16,512]{2,1,0:T(8,128)(2,1)S(1)}, bf16[4,16,512]{2,1,0:T(8,128)(2,1)S(1)}, u32[]{:S(2)}, u32[]{:S(2)}) collective-permute-start(bf16[4,16,512]{2,1,0:T(8,128)(2,1)S(1)} %bitcast.142), channel_id=1, source_target_pairs={{0,8},{8,16},{16,24},{24,0},{1,9},{9,17},{17,25},{25,1},{2,10},{10... | collective-permute-start | bytes 196616 | tf_op jit(solution)/shard_map/ppermute | solution.py:32
  78.8 37.9 %collective-permute-start.7 = (bf16[12,4,512]{2,1,0:T(4,128)(2,1)S(1)}, bf16[12,4,512]{2,1,0:T(4,128)(2,1)S(1)}, u32[]{:S(2)}, u32[]{:S(2)}) collective-permute-start(bf16[12,4,512]{2,1,0:T(4,128)(2,1)S(1)} %get-tuple-element.224), channel_id=1, source_target_pairs={{1,0},{2,1},{3,2},{4,3},{5,4},{6,5},{7,6},{0,7},{9,8},{10,9},{11,1... | collective-permute-start | bytes 147464 | tf_op jit(solution)/shard_map/ppermute | solution.py:34
  78.9 37.9 %collective-permute-start.6 = (bf16[12,4,512]{2,1,0:T(4,128)(2,1)S(1)}, bf16[12,4,512]{2,1,0:T(4,128)(2,1)S(1)}, u32[]{:S(2)}, u32[]{:S(2)}) collective-permute-start(bf16[12,4,512]{2,1,0:T(4,128)(2,1)S(1)} %get-tuple-element.223), channel_id=1, source_target_pairs={{0,1},{1,2},{2,3},{3,4},{4,5},{5,6},{6,7},{7,0},{8,9},{9,10},{10,1... | collective-permute-start | bytes 147464 | tf_op jit(solution)/shard_map/ppermute | solution.py:32
  132.9 7.3 %copy-start.1 = (f32[512,1536]{1,0:T(8,128)}, f32[512,1536]{1,0:T(8,128)S(1)}, u32[]{:S(2)}) copy-start(f32[512,1536]{1,0:T(8,128)S(1)} %fusion) | copy-start | bytes 9437188
  138.9 5.3 collective-permute-start.8
  143.5 129.1 %copy-start.2 = (f32[512,512]{0,1:T(8,128)}, f32[512,512]{0,1:T(8,128)S(1)}, u32[]{:S(2)}) copy-start(f32[512,512]{0,1:T(8,128)S(1)} %copy.41) | copy-start | bytes 3145732
  143.5 4.8 collective-permute-start.9
  144.1 408.6 %all-reduce.7.cloned.1.call-start = ((), (), s32[]{:S(2)}) async-start(), calls=%async_computation.1 | async-start | bytes 29622272 | tf_op jit(solution)/shard_map/psum | solution.py:229
  144.2 12.6 %copy-start.21 = (f32[64,1024]{1,0:T(8,128)S(1)}, f32[64,1024]{1,0:T(8,128)}, u32[]{:S(2)}) copy-start(f32[64,1024]{1,0:T(8,128)} %copy-done.20) | copy-start | bytes 786436
  145.1 124.5 %copy-start.30 = (f32[64,512]{1,0:T(8,128)S(1)}, f32[64,512]{1,0:T(8,128)}, u32[]{:S(2)}) copy-start(f32[64,512]{1,0:T(8,128)} %copy-done.29) | copy-start | bytes 393220
  149.2 4.6 collective-permute-start.11
  150.5 6.2 %collective-permute-start.10 = (bf16[4,16,512]{2,1,0:T(8,128)(2,1)S(1)}, bf16[4,16,512]{2,1,0:T(8,128)(2,1)S(1)}, u32[]{:S(2)}, u32[]{:S(2)}) collective-permute-start(bf16[4,16,512]{2,1,0:T(8,128)(2,1)S(1)} %get-tuple-element.221), channel_id=1, source_target_pairs={{8,0},{16,8},{24,16},{9,1},{17,9},{25,17},{10,2},{18,10},{26,18},{... | collective-permute-start | bytes 196616 | tf_op jit(solution)/shard_map/ppermute | solution.py:22
  153.8 118.8 %copy-start.36 = (f32[1,512]{1,0:T(1,128)S(1)}, f32[1,512]{1,0:T(1,128)}, u32[]{:S(2)}) copy-start(f32[1,512]{1,0:T(1,128)} %copy-done.35) | copy-start | bytes 6148
  153.8 118.8 %copy-start.38 = (f32[512]{0:T(512)S(1)}, f32[512]{0:T(512)}, u32[]{:S(2)}) copy-start(f32[512]{0:T(512)} %copy-done.37) | copy-start | bytes 6148
  153.8 118.9 %copy-start.42 = (f32[512]{0:T(512)S(1)}, f32[512]{0:T(512)}, u32[]{:S(2)}) copy-start(f32[512]{0:T(512)} %copy-done.40) | copy-start | bytes 6148
  279.9 3.3 copy-start.48
  287.1 5.5 copy-start.45
  287.1 5.5 copy-start.55
  287.1 5.5 copy-start.56
  287.1 5.5 copy-start.57
  289.5 53.1 %collective-permute-start.12 = (bf16[12,4,512]{2,1,0:T(4,128)(2,1)S(1)}, bf16[12,4,512]{2,1,0:T(4,128)(2,1)S(1)}, u32[]{:S(2)}, u32[]{:S(2)}) collective-permute-start(bf16[12,4,512]{2,1,0:T(4,128)(2,1)S(1)} %get-tuple-element.216), channel_id=1, source_target_pairs={{0,7},{1,0},{2,1},{3,2},{4,3},{5,4},{6,5},{7,6},{8,15},{9,8},{10,9... | collective-permute-start | bytes 147464 | tf_op jit(solution)/shard_map/ppermute | solution.py:16
  289.7 54.5 %collective-permute-start.13 = (bf16[12,4,512]{2,1,0:T(4,128)(2,1)S(1)}, bf16[12,4,512]{2,1,0:T(4,128)(2,1)S(1)}, u32[]{:S(2)}, u32[]{:S(2)}) collective-permute-start(bf16[12,4,512]{2,1,0:T(4,128)(2,1)S(1)} %get-tuple-element.215), channel_id=1, source_target_pairs={{0,1},{1,2},{2,3},{3,4},{4,5},{5,6},{6,7},{7,0},{8,9},{9,10},{10,1... | collective-permute-start | bytes 147464 | tf_op jit(solution)/shard_map/ppermute | solution.py:16
  334.6 4.6 copy-start.4
  346.9 6.0 %collective-permute-start.15 = (bf16[4,16,512]{2,1,0:T(8,128)(2,1)S(1)}, bf16[4,16,512]{2,1,0:T(8,128)(2,1)S(1)}, u32[]{:S(2)}, u32[]{:S(2)}) collective-permute-start(bf16[4,16,512]{2,1,0:T(8,128)(2,1)S(1)} %get-tuple-element.220), channel_id=1, source_target_pairs={{0,8},{8,16},{16,24},{1,9},{9,17},{17,25},{2,10},{10,18},{18,26},{... | collective-permute-start | bytes 196616 | tf_op jit(solution)/shard_map/ppermute | solution.py:22
  349.4 7.8 %collective-permute-start.14 = (bf16[4,16,512]{2,1,0:T(8,128)(2,1)S(1)}, bf16[4,16,512]{2,1,0:T(8,128)(2,1)S(1)}, u32[]{:S(2)}, u32[]{:S(2)}) collective-permute-start(bf16[4,16,512]{2,1,0:T(8,128)(2,1)S(1)} %get-tuple-element.219), channel_id=1, source_target_pairs={{8,0},{16,8},{24,16},{9,1},{17,9},{25,17},{10,2},{18,10},{26,18},{... | collective-permute-start | bytes 196616 | tf_op jit(solution)/shard_map/ppermute | solution.py:22
  553.5 6.5 %copy-start.28 = (f32[64,512]{1,0:T(8,128)}, f32[64,512]{1,0:T(8,128)S(1)}, u32[]{:S(2)}) copy-start(f32[64,512]{1,0:T(8,128)S(1)} %fusion.101) | copy-start | bytes 393220
  553.5 6.5 %copy-start.18 = (f32[1,512,512]{2,1,0:T(8,128)S(1)}, f32[1,512,512]{2,1,0:T(8,128)}, u32[]{:S(2)}) copy-start(f32[1,512,512]{2,1,0:T(8,128)} %get-tuple-element.209) | copy-start | bytes 3145732
  553.5 6.5 %copy-start.19 = (f32[1,512,512]{2,1,0:T(8,128)S(1)}, f32[1,512,512]{2,1,0:T(8,128)}, u32[]{:S(2)}) copy-start(f32[1,512,512]{2,1,0:T(8,128)} %get-tuple-element.210) | copy-start | bytes 3145732
  (35 other events, 64.8 us)
Sparse Core Ops, SparseCore 0:
  144.2 123.7 all-reduce.4
  287.2 265.4 all-reduce.6
where the time goes:
time: 575 us; the launch traced here: 574 us
  waiting for transfers between devices  317 us (55%)
  blocking collectives  118 us (21%)
  matrix products  40.5 us (7%)
  other arithmetic  33.4 us (6%)
  local copies, waits for them, and re-layouts  31 us (5%)
  starting transfers between devices  17.3 us (3%)
  between operations  15.9 us (3%)
    psum x2, waiting for transfers between devices, local(): lax.psum((layer_grads[0], layer_grads[1], layer_grads[2], layer_grads[3],...  302 us
    all_gather x2, blocking collectives, local(): coarse = lax.all_gather(state[:CO], ('band', 'sector'), axis=0, tiled=True)  76.5 us
    psum x1, blocking collectives, local(): lax.psum((layer_grads[0], layer_grads[1], layer_grads[2], layer_grads[3],...  42 us
    unnamed x140, local copies, waits for them, and re-layouts  13.2 us
  transfers between devices with their start and end apart: 18, of which 8 were waited for; matrix products, arithmetic and copies ran while one was open for 7% of the time, Pallas kernels for 0%

commit v1 on v0

v1 whole, which is shorter than its diff:
```python
import math

import jax
import jax.numpy as jnp
from jax import lax
from jax.sharding import PartitionSpec as P

CO = 2
PIECES = 32
EPSILON = 1e-05
F32 = jnp.float32
BF16 = jnp.bfloat16


def moved(value, axis, by):
    count = lax.axis_size(axis)
    return lax.ppermute(value, axis, [(i, (i + by) % count) for i in range(count)])


def swapped(value, stage):
    axis, bit = stage
    return lax.ppermute(value, axis, [(i, i ^ bit) for i in range(lax.axis_size(axis))])


def axis_bits(axis):
    return [(axis, 1 << k) for k in range(lax.axis_size(axis).bit_length() - 1)]


def added(first, second):
    return (first.astype(F32) + second.astype(F32)).astype(BF16)


def scatter_sum(pieces, order):
    half = pieces.shape[0] // 2
    keep, send = pieces[:half], pieces[half:]
    for step, stage in enumerate(order):
        recv = swapped(send, stage)
        if half == 1:
            return added(keep, recv)
        half //= 2
        send = added(keep[half:], recv[half:])
        keep = added(keep[:half], recv[:half])


def gathered(piece, order):
    for stage in reversed(order):
        piece = jnp.concatenate([piece, swapped(piece, stage)], axis=0)
    return piece


def stage_orders():
    sector, band = axis_bits("sector"), axis_bits("band")
    depth = PIECES.bit_length() - 1
    first = sector + band
    second = sector[:1] + sector[1:][::-1] + band
    return (first[:depth], second[:depth]), first[depth:]


def summed_pieces(pieces):
    orders, rest = stage_orders()
    outs = []
    for part, order in enumerate(orders):
        own = scatter_sum(pieces[part], order)
        for stage in rest:
            own = added(own, swapped(own, stage))
        outs.append(gathered(own, order))
    return outs


def relative_index():
    orders, _ = stage_orders()
    table = []
    for order in orders:
        index = jnp.zeros((PIECES,), jnp.int32)
        span = PIECES
        for k, (axis, bit) in enumerate(order):
            span //= 2
            own = (lax.axis_index(axis) // bit) % 2
            position = (jnp.arange(PIECES, dtype=jnp.int32) // span) % 2
            index = index + (own ^ position) * span
        table.append(index)
    return table


def summed_vectors(values):
    for stage in axis_bits("sector") + axis_bits("band"):
        values = values + swapped(values, stage)
    return values


def sender_rows(senders, lat, lon, payload, own_rows):
    bands, sectors = lax.axis_size("band"), lax.axis_size("sector")
    width = lon + 2 * lat
    ext = 3 * lat * width
    row, col = senders // width, senders % width
    block, row = row // lat, row % lat
    base = jnp.where(block == 1, 0, jnp.where(block == 0, payload, 2 * payload))
    rim = lat * lat
    inside = jnp.where(
        col < lat,
        own_rows + row * lat + col,
        jnp.where(col < lat + lon, row * lon + col - lat, own_rows + rim + row * lat + col - lat - lon),
    )
    coarse = senders - ext
    owner, item = coarse // CO, coarse % CO
    away = (owner // sectors - lax.axis_index("band") + bands) % bands
    spot = (owner % sectors) * CO + item
    head = own_rows + 2 * rim
    coarse_row = jnp.where(
        away == 0,
        head + spot,
        jnp.where(
            away == bands - 1,
            payload + head + spot,
            jnp.where(away == 1, 2 * payload + head + spot, 3 * payload + (away - 2) * sectors * CO + spot),
        ),
    )
    return jnp.where(senders < ext, base + inside, coarse_row)


def collected(state, lat, lon):
    width = state.shape[-1]
    grid = state.reshape(lat, lon, width)
    sectors, bands = lax.axis_size("sector"), lax.axis_size("band")
    here = lax.axis_index("sector")
    rims = jnp.concatenate([grid[:, :lat], grid[:, lon - lat :]], axis=1)
    around = lax.all_gather(rims, "sector")
    west = lax.dynamic_index_in_dim(around, (here + sectors - 1) % sectors, 0, False)[:, lat:]
    east = lax.dynamic_index_in_dim(around, (here + 1) % sectors, 0, False)[:, :lat]
    coarse = around[:, 0, :CO].reshape(sectors * CO, width)
    payload = jnp.concatenate(
        [state, west.reshape(lat * lat, width), east.reshape(lat * lat, width), coarse], axis=0
    )
    north = moved(payload, "band", 1)
    south = moved(payload, "band", -1)
    others = [moved(coarse, "band", -away) for away in range(2, bands - 1)]
    return jnp.concatenate([payload, north, south] + others, axis=0)


def returned(table_grad, lat, lon, payload):
    width = table_grad.shape[-1]
    sectors, bands = lax.axis_size("sector"), lax.axis_size("band")
    own_rows, rim = lat * lon, lat * lat
    low = table_grad[payload:].astype(BF16)
    head = own_rows + 2 * rim
    from_south = moved(low[:payload], "band", -1)
    from_north = moved(low[payload : 2 * payload], "band", 1)
    total = table_grad[:payload] + from_south.astype(F32) + from_north.astype(F32)
    coarse = total[head:]
    for away in range(2, bands - 1):
        start = 2 * payload + (away - 2) * sectors * CO
        coarse = coarse + moved(low[start : start + sectors * CO], "band", away).astype(F32)
    rims = total[own_rows:head].astype(BF16)
    from_east = moved(rims[:rim], "sector", -1).astype(F32).reshape(lat, lat, width)
    from_west = moved(rims[rim:], "sector", 1).astype(F32).reshape(lat, lat, width)
    spread = lax.all_to_all(
        coarse.astype(BF16).reshape(sectors, CO, width), "sector", 0, 0, tiled=True
    )
    mine = jnp.sum(spread.astype(F32), axis=0)
    grid = total[:own_rows].reshape(lat, lon, width)
    grid = grid.at[:, lon - lat :].add(from_east).at[:, :lat].add(from_west)
    return grid.reshape(own_rows, width).at[:CO].add(mine)


def mlp_forward(inputs, first_weight, first_bias, second_weight, norm_gain):
    pre_act = jnp.dot(inputs, first_weight, preferred_element_type=F32) + first_bias
    sigmoid_val = jax.nn.sigmoid(pre_act)
    activated = (pre_act * sigmoid_val).astype(BF16)
    mixed = jnp.dot(activated, second_weight, preferred_element_type=F32)
    centered = mixed - jnp.mean(mixed, axis=-1, keepdims=True)
    inv_std = lax.rsqrt(jnp.mean(centered * centered, axis=-1, keepdims=True) + EPSILON)
    normed = centered * inv_std
    return (normed * norm_gain, (inputs, pre_act, sigmoid_val, activated, normed, inv_std))


def mlp_backward(grad_out, saved, first_weight, second_weight, norm_gain):
    inputs, pre_act, sigmoid_val, activated, normed, inv_std = saved
    grad_gain = jnp.sum(grad_out * normed, axis=0)
    grad_normed = grad_out * norm_gain
    grad_mixed = inv_std * (
        grad_normed
        - jnp.mean(grad_normed, axis=-1, keepdims=True)
        - normed * jnp.mean(grad_normed * normed, axis=-1, keepdims=True)
    )
    mixed_low = grad_mixed.astype(BF16)
    grad_second = lax.dot_general(
        activated, mixed_low, (((0,), (0,)), ((), ())), preferred_element_type=F32
    )
    grad_act = lax.dot_general(
        mixed_low, second_weight, (((1,), (1,)), ((), ())), preferred_element_type=F32
    )
    grad_pre = grad_act * sigmoid_val * (1.0 + pre_act * (1.0 - sigmoid_val))
    grad_bias = jnp.sum(grad_pre, axis=0)
    pre_low = grad_pre.astype(BF16)
    grad_first = lax.dot_general(
        inputs, pre_low, (((0,), (0,)), ((), ())), preferred_element_type=F32
    )
    grad_inputs = lax.dot_general(
        pre_low, first_weight, (((1,), (1,)), ((), ())), preferred_element_type=F32
    )
    return (grad_inputs, (grad_first, grad_bias, grad_second, grad_gain))


def picked(onehot, rows, transpose=False):
    dims = (((0,), (0,)), ((), ())) if transpose else (((1,), (0,)), ((), ()))
    high = rows.astype(BF16)
    low = (rows - high.astype(F32)).astype(BF16)
    out = lax.dot_general(onehot, high, dims, preferred_element_type=F32)
    return out + lax.dot_general(onehot, low, dims, preferred_element_type=F32)


def local(
    node_states,
    edge_states,
    senders,
    receivers,
    edge_count,
    edge_hidden,
    edge_offset,
    edge_output,
    edge_scale,
    node_hidden,
    node_offset,
    node_output,
    node_scale,
    output_cotangent,
):
    lat, lon, width = node_states.shape
    own_rows = lat * lon
    slots = edge_states.shape[1]
    depth = edge_hidden.shape[0]
    sectors, bands = lax.axis_size("sector"), lax.axis_size("band")
    payload = own_rows + 2 * lat * lat + sectors * CO
    table_rows = 3 * payload + (bands - 3) * sectors * CO
    edge_rows = edge_states[0]
    recv_index = receivers[0]
    send_index = sender_rows(senders[0], lat, lon, payload, own_rows)
    live_mask = (jnp.arange(slots, dtype=jnp.int32) < edge_count[0]).astype(F32)[:, None]
    incidence = (recv_index[:, None] == jnp.arange(own_rows, dtype=jnp.int32)[None, :]).astype(BF16)
    sender_onehot = (
        send_index[:, None] == jnp.arange(table_rows, dtype=jnp.int32)[None, :]
    ).astype(BF16)
    state = node_states.reshape(own_rows, width)
    records = []
    for step in range(depth):
        table = collected(state, lat, lon)
        sent = jnp.dot(sender_onehot, table, preferred_element_type=F32).astype(BF16)
        received = jnp.dot(incidence, state, preferred_element_type=F32).astype(BF16)
        inputs = jnp.concatenate([edge_rows, sent, received], axis=1)
        result, edge_saved = mlp_forward(
            inputs, edge_hidden[step], edge_offset[step], edge_output[step], edge_scale[step]
        )
        update = result * live_mask
        total = picked(incidence, update, True)
        node_inputs = jnp.concatenate([state, total.astype(BF16)], axis=1)
        node_delta, node_saved = mlp_forward(
            node_inputs, node_hidden[step], node_offset[step], node_output[step], node_scale[step]
        )
        records.append((edge_saved, node_saved))
        edge_rows = (edge_rows.astype(F32) + update).astype(BF16)
        state = (state.astype(F32) + node_delta).astype(BF16)
    node_result = state.reshape(lat, lon, width)
    grad_state = output_cotangent.reshape(own_rows, width).astype(F32)
    grad_edges = jnp.zeros((slots, width), F32)
    vectors = [None] * depth
    sums = [None] * depth
    index = relative_index()
    for step in reversed(range(depth)):
        edge_saved, node_saved = records[step]
        grad_in, node_grads = mlp_backward(
            grad_state, node_saved, node_hidden[step], node_output[step], node_scale[step]
        )
        grad_state = grad_state + grad_in[:, :width]
        flow_grad = (picked(incidence, grad_in[:, width:]) + grad_edges) * live_mask
        grad_inputs, edge_grads = mlp_backward(
            flow_grad, edge_saved, edge_hidden[step], edge_output[step], edge_scale[step]
        )
        grad_edges = grad_edges + grad_inputs[:, :width]
        grad_state = grad_state + picked(incidence, grad_inputs[:, 2 * width :], True)
        table_grad = picked(sender_onehot, grad_inputs[:, width : 2 * width], True)
        grad_state = grad_state + returned(table_grad, lat, lon, payload)
        stacked = jnp.concatenate([edge_grads[0], edge_grads[2], node_grads[0], node_grads[2]], axis=0)
        stacked = stacked.astype(BF16).reshape(-1, PIECES, width // PIECES, width)
        stacked = jnp.moveaxis(stacked, 1, 0)
        half = width // 2
        parts = jnp.stack(
            [
                jnp.take(stacked[..., part * half : (part + 1) * half], index[part], axis=0)
                for part in range(2)
            ]
        )
        sums[step] = summed_pieces(parts)
        vectors[step] = jnp.stack([edge_grads[1], edge_grads[3], node_grads[1], node_grads[3]])
    vectors = summed_vectors(jnp.stack(vectors))
    factor = 1.0 / math.sqrt(own_rows * bands * sectors)
    matrices = []
    for step in range(depth):
        halves = [jnp.take(sums[step][part], index[part], axis=0) for part in range(2)]
        whole = jnp.concatenate(halves, axis=-1)
        whole = jnp.moveaxis(whole, 0, 1).reshape(-1, width).astype(F32) * factor
        matrices.append(whole)
    matrices = jnp.stack(matrices)
    vectors = vectors * factor
    return (
        node_result,
        grad_state.reshape(lat, lon, width),
        grad_edges[None],
        matrices[:, : 3 * width],
        vectors[:, 0],
        matrices[:, 3 * width : 4 * width],
        vectors[:, 1],
        matrices[:, 4 * width : 6 * width],
        vectors[:, 2],
        matrices[:, 6 * width :],
        vectors[:, 3],
    )


def solution(mesh):
    grid = P("band", "sector", None)
    edges = P(("band", "sector"), None, None)
    index = P(("band", "sector"), None)
    return jax.shard_map(
        local,
        mesh=mesh,
        in_specs=(grid, edges, index, index, P(("band", "sector"))) + (P(),) * 8 + (grid,),
        out_specs=(grid, grid, edges) + (P(),) * 8,
        check_vma=False,
    )
```

time: 575 us -> 350 us (0.61)
  waiting for transfers between devices: 317 us -> 80.3 us
  blocking collectives: 118 us -> 20.1 us
  starting transfers between devices: 17.3 us -> 73.6 us
  local copies, waits for them, and re-layouts: 31 us -> 85.5 us
  other arithmetic: 33.4 us -> 47.4 us
  between operations: 15.9 us -> 3.49 us
  matrix products: 40.5 us -> 33.3 us
    psum x2 -> x0, waiting for transfers between devices: 302 us -> none  [local(): lax.psum((layer_grads[0], layer_grads[1], layer_grads[2], layer_grads[3],...]
    ppermute x16 -> x61, waiting for transfers between devices: 14.9 us -> 78.5 us  [the longest x45 71.3 us: swapped(): lax.ppermute(value, axis, [(i, i ^ bit) for i in range(lax.axis_size(axis...]
    all_gather x2, blocking collectives: 76.5 us -> 20.1 us  [collected(): around = lax.all_gather(rims, 'sector')]
    ppermute x16 -> x61, starting transfers between devices: 17.2 us -> 66.7 us  [the longest x45 43.3 us: swapped(): lax.ppermute(value, axis, [(i, i ^ bit) for i in range(lax.axis_size(axis...]
    psum x1 -> x0, blocking collectives: 42 us -> none  [local(): lax.psum((layer_grads[0], layer_grads[1], layer_grads[2], layer_grads[3],...]
    unnamed x140 -> x198, local copies, waits for them, and re-layouts: 13.2 us -> 29.9 us
    mul x8 -> x3, other arithmetic: 14.5 us -> 2.18 us  [the longest x2 2.16 us: local(): whole = jnp.moveaxis(whole, 0, 1).reshape(-1, width).astype(F32) * factor]
    gather x8, local copies, waits for them, and re-layouts: 9.67 us -> 21.7 us  [the longest x4 11.5 us: local(): jnp.take(stacked[..., part * half:(part + 1) * half], index[part], axis=0)]
  transfers between devices with their start and end apart: 18 -> 63, of which waited for: 8 -> 33; matrix products, arithmetic and copies ran while one was open for 7% -> 31% of each run, Pallas kernels for 0% -> 0%
where the time goes in v1:
time: 350 us; the launch traced here: 344 us
  local copies, waits for them, and re-layouts  85.5 us (24%)
  waiting for transfers between devices  80.3 us (23%)
  starting transfers between devices  73.6 us (21%)
  other arithmetic  47.4 us (14%)
  matrix products  33.3 us (10%)
  blocking collectives  20.1 us (6%)
    ppermute x45, waiting for transfers between devices, swapped(): lax.ppermute(value, axis, [(i, i ^ bit) for i in range(lax.axis_size(axis...  71.3 us
    ppermute x45, starting transfers between devices, swapped(): lax.ppermute(value, axis, [(i, i ^ bit) for i in range(lax.axis_size(axis...  43.3 us
    unnamed x198, local copies, waits for them, and re-layouts  29.9 us
    ppermute x16, starting transfers between devices, moved(): lax.ppermute(value, axis, [(i, (i + by) % count) for i in range(count)])  23.4 us
    all_gather x2, blocking collectives, collected(): around = lax.all_gather(rims, 'sector')  20.1 us
    gather x4, local copies, waits for them, and re-layouts, local(): jnp.take(stacked[..., part * half:(part + 1) * half], index[part], axis=0)  11.5 us
    gather x4, local copies, waits for them, and re-layouts, local(): jnp.take(sums[step][part], index[part], axis=0)  10.2 us
    another operation x3, other arithmetic, local(): matrices = jnp.stack(matrices)  8.31 us
  transfers between devices with their start and end apart: 63, of which 33 were waited for; matrix products, arithmetic and copies ran while one was open for 31% of the time, Pallas kernels for 0%

profile of v1, /device:TPU:0, one launch (start us, length us, event | category | flops | bytes accessed | tf_op | source)
XLA Modules:
  0.0 343.8 jit_solution(7232216785515613147)
XLA Ops:
  1.5 10.8 %all-gather = bf16[32,8,512]{2,1,0:T(8,128)(2,1)S(1)} all-gather(bf16[4,8,512]{2,1,0:T(8,128)(2,1)S(1)} %pad_maximum_fusion.29), channel_id=2, replica_groups=mesh['band'=4,'sector'=8] {'sector'}, dimensions={0}, use_global_device_ids=true | all-gather | bytes 294912 | tf_op jit(solution)/shard_map/all_gather | solution.py:127
  12.3 2.7 collective-permute-start.2
  32.0 2.1 convolution_convert_fusion.11
  36.0 2.1 copy.39
  43.0 2.4 fusion.20
  50.5 9.3 %all-gather.1 = bf16[32,8,512]{2,1,0:T(8,128)(2,1)S(1)} all-gather(bf16[4,8,512]{2,1,0:T(8,128)(2,1)S(1)} %pad_maximum_fusion.30), channel_id=3, replica_groups=mesh['band'=4,'sector'=8] {'sector'}, dimensions={0}, use_global_device_ids=true | all-gather | bytes 294912 | tf_op jit(solution)/shard_map/all_gather | solution.py:127
  61.1 3.0 collective-permute-start.4
  66.2 4.7 %collective-permute-done.3 = bf16[112,512]{1,0:T(8,128)(2,1)S(1)} collective-permute-done((bf16[112,512]{1,0:T(8,128)(2,1)S(1)}, bf16[112,512]{1,0:T(8,128)(2,1)S(1)}, u32[]{:S(2)}, u32[]{:S(2)}) %collective-permute-start.3) | collective-permute-done | bytes 114720 | tf_op jit(solution)/shard_map/ppermute | solution.py:17
  89.4 3.5 %gather_fusion.4 = bf16[32,7,16,256]{3,2,1,0:T(8,128)(2,1)} fusion(bf16[32,7,16,256]{3,2,0,1:T(8,128)(2,1)} %get-tuple-element.148, s32[1024]{0:T(1024)} %pad_clamp_fusion.1), kind=kCustom, calls=%fused_computation.4.clone | custom fusion | bytes 3670144 | tf_op jit(solution)/shard_map/jit(_take)/gather | solution.py:288
  99.0 2.1 gather_fusion.6
  109.7 3.3 all-to-all-start
  113.6 2.5 collective-permute-start.8
  130.9 2.5 fusion.161
  136.1 2.4 collective-permute-start.57
  142.2 3.7 %gather_fusion = bf16[32,7,16,256]{3,2,1,0:T(8,128)(2,1)} fusion(bf16[32,7,16,256]{3,2,0,1:T(8,128)(2,1)} %get-tuple-element.150, s32[1024]{0:T(1024)} %pad_clamp_fusion.1), kind=kCustom, calls=%fused_computation.clone | custom fusion | bytes 3670144 | tf_op jit(solution)/shard_map/jit(_take)/gather | solution.py:288
  145.9 2.1 gather_fusion.2
  153.6 2.2 add_convert_fusion.4
  156.8 2.2 add_convert_fusion.2
  164.0 2.6 collective-permute-done.37
  168.0 4.2 %collective-permute-done.47 = bf16[8,7,16,256]{3,2,1,0:T(8,128)(2,1)S(1)} collective-permute-done((bf16[8,7,16,256]{3,2,1,0:T(8,128)(2,1)}, bf16[8,7,16,256]{3,2,1,0:T(8,128)(2,1)S(1)}, u32[]{:S(2)}, u32[]{:S(2)}) %collective-permute-start.47) | collective-permute-done | bytes 458784 | tf_op jit(solution)/shard_map/ppermute | solution.py:22
  176.1 2.3 collective-permute-done.48
  184.8 2.7 collective-permute-done.40
  189.2 2.6 collective-permute-start.51
  194.3 2.4 collective-permute-start.52
  201.5 5.4 %collective-permute-done.43 = bf16[4,7,16,256]{3,2,1,0:T(8,128)(2,1)S(1)} collective-permute-done((bf16[4,7,16,256]{3,2,1,0:T(8,128)(2,1)S(1)}, bf16[4,7,16,256]{3,2,1,0:T(8,128)(2,1)S(1)}, u32[]{:S(2)}, u32[]{:S(2)}) %collective-permute-start.43) | collective-permute-done | bytes 229408 | tf_op jit(solution)/shard_map/ppermute | solution.py:22
  211.1 4.4 %collective-permute-done.44 = bf16[8,7,16,256]{3,2,1,0:T(8,128)(2,1)S(1)} collective-permute-done((bf16[8,7,16,256]{3,2,1,0:T(8,128)(2,1)S(1)}, bf16[8,7,16,256]{3,2,1,0:T(8,128)(2,1)S(1)}, u32[]{:S(2)}, u32[]{:S(2)}) %collective-permute-start.44) | collective-permute-done | bytes 458784 | tf_op jit(solution)/shard_map/ppermute | solution.py:22
  218.1 2.0 collective-permute-done.60
  223.2 3.6 %all-to-all-start.1 = ((bf16[8,2,512]{2,1,0:T(2,128)(2,1)}), bf16[8,2,512]{2,1,0:T(2,128)(2,1)S(1)}, u32[]{:S(2)}, u32[]{:S(2)}) async-start(bf16[8,2,512]{2,1,0:T(2,128)(2,1)} %reshape.570), calls=%async_computation.1 | async-start | bytes 32768 | tf_op jit(solution)/shard_map/all_to_all | solution.py:156
  228.9 2.2 constant_dynamic-update-slice_fusion.52
  231.1 3.6 %gather_fusion.7 = bf16[32,7,16,256]{3,2,1,0:T(8,128)(2,1)} fusion(bf16[32,7,16,256]{3,2,1,0:T(8,128)(2,1)} %constant_dynamic-update-slice_fusion.52, s32[1024]{0:T(1024)} %pad_clamp_fusion), kind=kCustom, calls=%fused_computation.7.clone | custom fusion | bytes 3670144 | tf_op jit(solution)/shard_map/jit(_take)/gather | solution.py:298
  234.7 3.3 broadcast_select_fusion.5
  242.8 2.6 collective-permute-start.13
  252.4 9.2 %collective-permute-done.17 = bf16[8,7,16,256]{3,2,1,0:T(8,128)(2,1)S(1)} collective-permute-done((bf16[8,7,16,256]{3,2,1,0:T(8,128)(2,1)S(1)}, bf16[8,7,16,256]{3,2,1,0:T(8,128)(2,1)S(1)}, u32[]{:S(2)}, u32[]{:S(2)}) %collective-permute-start.17) | collective-permute-done | bytes 458784 | tf_op jit(solution)/shard_map/ppermute | solution.py:22
  265.6 4.4 %collective-permute-done.18 = bf16[4,7,16,256]{3,2,1,0:T(8,128)(2,1)S(1)} collective-permute-done((bf16[4,7,16,256]{3,2,1,0:T(8,128)(2,1)S(1)}, bf16[4,7,16,256]{3,2,1,0:T(8,128)(2,1)S(1)}, u32[]{:S(2)}, u32[]{:S(2)}) %collective-permute-start.18) | collective-permute-done | bytes 229408 | tf_op jit(solution)/shard_map/ppermute | solution.py:22
  272.2 3.4 collective-permute-done.19
  278.7 4.8 %collective-permute-done.20 = bf16[1,7,16,256]{3,2,1,0:T(8,128)(2,1)S(1)} collective-permute-done((bf16[1,7,16,256]{3,2,1,0:T(8,128)(2,1)S(1)}, bf16[1,7,16,256]{3,2,1,0:T(8,128)(2,1)S(1)}, u32[]{:S(2)}, u32[]{:S(2)}) %collective-permute-start.20) | collective-permute-done | bytes 57376 | tf_op jit(solution)/shard_map/ppermute | solution.py:22
  285.4 2.4 collective-permute-start.31
  290.5 2.1 collective-permute-start.32
  292.6 2.3 collective-permute-done.22
  296.6 4.3 %collective-permute-done.23 = bf16[4,7,16,256]{3,2,1,0:T(8,128)(2,1)S(1)} collective-permute-done((bf16[4,7,16,256]{3,2,1,0:T(8,128)(2,1)S(1)}, bf16[4,7,16,256]{3,2,1,0:T(8,128)(2,1)S(1)}, u32[]{:S(2)}, u32[]{:S(2)}) %collective-permute-start.23) | collective-permute-done | bytes 229408 | tf_op jit(solution)/shard_map/ppermute | solution.py:22
  302.4 2.2 collective-permute-done.33
  307.0 4.4 %collective-permute-done.24 = bf16[8,7,16,256]{3,2,1,0:T(8,128)(2,1)S(1)} collective-permute-done((bf16[8,7,16,256]{3,2,1,0:T(8,128)(2,1)S(1)}, bf16[8,7,16,256]{3,2,1,0:T(8,128)(2,1)S(1)}, u32[]{:S(2)}, u32[]{:S(2)}) %collective-permute-start.24) | collective-permute-done | bytes 458784 | tf_op jit(solution)/shard_map/ppermute | solution.py:22
  317.4 4.7 %copy.44 = f32[7,32,16,512]{3,2,1,0:T(8,128)} copy(f32[7,32,16,512]{3,2,0,1:T(8,128)S(1)} %multiply_bitcast_fusion) | data formatting | bytes 14680064 | tf_op jit(solution)/shard_map/mul | solution.py:300
  323.1 2.3 gather_fusion.1
  327.9 2.3 gather_fusion.3
  335.0 2.5 fusion.1
  337.5 2.4 pad_maximum_fusion.2
  339.9 3.4 fusion
  (493 shorter events, 175.6 us)
Async XLA Ops:
  12.3 27.8 %collective-permute-start.2 = (bf16[16,512]{1,0:T(8,128)(2,1)S(1)}, bf16[16,512]{1,0:T(8,128)(2,1)}, u32[]{:S(2)}, u32[]{:S(2)}) collective-permute-start(bf16[16,512]{1,0:T(8,128)(2,1)S(1)} %reshape_squeeze.6), channel_id=1, source_target_pairs={{0,16},{8,24},{16,0},{24,8},{1,17},{9,25},{17,1},{25,9},{2,18},{10... | collective-permute-start | bytes 49160 | tf_op jit(solution)/shard_map/ppermute | solution.py:17
  15.9 23.5 %collective-permute-start.1 = (bf16[112,512]{1,0:T(8,128)(2,1)S(1)}, bf16[112,512]{1,0:T(8,128)(2,1)S(1)}, u32[]{:S(2)}, u32[]{:S(2)}) collective-permute-start(bf16[112,512]{1,0:T(8,128)(2,1)S(1)} %pad_maximum_fusion.19), channel_id=1, source_target_pairs={{0,24},{8,0},{16,8},{24,16},{1,25},{9,1},{17,9},{25,17},{2,26},{10... | collective-permute-start | bytes 344072 | tf_op jit(solution)/shard_map/ppermute | solution.py:17
  17.2 21.5 %collective-permute-start = (bf16[112,512]{1,0:T(8,128)(2,1)S(1)}, bf16[112,512]{1,0:T(8,128)(2,1)S(1)}, u32[]{:S(2)}, u32[]{:S(2)}) collective-permute-start(bf16[112,512]{1,0:T(8,128)(2,1)S(1)} %pad_maximum_fusion.19), channel_id=1, source_target_pairs={{0,8},{8,16},{16,24},{24,0},{1,9},{9,17},{17,25},{25,1},{2,10},{10... | collective-permute-start | bytes 344072 | tf_op jit(solution)/shard_map/ppermute | solution.py:17
  60.0 10.9 %collective-permute-start.5 = (bf16[16,512]{1,0:T(8,128)(2,1)S(1)}, bf16[16,512]{1,0:T(8,128)(2,1)S(1)}, u32[]{:S(2)}, u32[]{:S(2)}) collective-permute-start(bf16[16,512]{1,0:T(8,128)(2,1)S(1)} %reshape_squeeze.7), channel_id=1, source_target_pairs={{0,16},{8,24},{16,0},{24,8},{1,17},{9,25},{17,1},{25,9},{2,18},{10... | collective-permute-start | bytes 49160 | tf_op jit(solution)/shard_map/ppermute | solution.py:17
  61.1 9.8 %collective-permute-start.4 = (bf16[112,512]{1,0:T(8,128)(2,1)S(1)}, bf16[112,512]{1,0:T(8,128)(2,1)S(1)}, u32[]{:S(2)}, u32[]{:S(2)}) collective-permute-start(bf16[112,512]{1,0:T(8,128)(2,1)S(1)} %pad_maximum_fusion.20), channel_id=1, source_target_pairs={{0,24},{8,0},{16,8},{24,16},{1,25},{9,1},{17,9},{25,17},{2,26},{10... | collective-permute-start | bytes 344072 | tf_op jit(solution)/shard_map/ppermute | solution.py:17
  64.1 6.8 %collective-permute-start.3 = (bf16[112,512]{1,0:T(8,128)(2,1)S(1)}, bf16[112,512]{1,0:T(8,128)(2,1)S(1)}, u32[]{:S(2)}, u32[]{:S(2)}) collective-permute-start(bf16[112,512]{1,0:T(8,128)(2,1)S(1)} %pad_maximum_fusion.20), channel_id=1, source_target_pairs={{0,8},{8,16},{16,24},{24,0},{1,9},{9,17},{17,25},{25,1},{2,10},{10... | collective-permute-start | bytes 344072 | tf_op jit(solution)/shard_map/ppermute | solution.py:17
  97.0 56.6 %collective-permute-start.36 = (bf16[16,7,16,256]{3,2,1,0:T(8,128)(2,1)}, bf16[16,7,16,256]{3,2,1,0:T(8,128)(2,1)}, u32[]{:S(2)}, u32[]{:S(2)}) collective-permute-start(bf16[16,7,16,256]{3,2,1,0:T(8,128)(2,1)} %slice.804), channel_id=1, source_target_pairs={{0,1},{1,0},{2,3},{3,2},{4,5},{5,4},{6,7},{7,6},{8,9},{9,8},{10,11... | collective-permute-start | bytes 2752520 | tf_op jit(solution)/shard_map/ppermute | solution.py:22
  97.0 9.5 %collective-permute-start.6 = (bf16[112,512]{1,0:T(8,128)(2,1)S(1)}, bf16[112,512]{1,0:T(8,128)(2,1)S(1)}, u32[]{:S(2)}, u32[]{:S(2)}) collective-permute-start(bf16[112,512]{1,0:T(8,128)(2,1)S(1)} %copy-done.39), channel_id=1, source_target_pairs={{0,24},{8,0},{16,8},{24,16},{1,25},{9,1},{17,9},{25,17},{2,26},{10... | collective-permute-start | bytes 344072 | tf_op jit(solution)/shard_map/ppermute | solution.py:17
  98.8 7.7 %collective-permute-start.7 = (bf16[112,512]{1,0:T(8,128)(2,1)S(1)}, bf16[112,512]{1,0:T(8,128)(2,1)S(1)}, u32[]{:S(2)}, u32[]{:S(2)}) collective-permute-start(bf16[112,512]{1,0:T(8,128)(2,1)S(1)} %copy-done.38), channel_id=1, source_target_pairs={{0,8},{8,16},{16,24},{24,0},{1,9},{9,17},{17,25},{25,1},{2,10},{10... | collective-permute-start | bytes 344072 | tf_op jit(solution)/shard_map/ppermute | solution.py:17
  104.1 52.7 %collective-permute-start.46 = (bf16[16,7,16,256]{3,2,1,0:T(8,128)(2,1)}, bf16[16,7,16,256]{3,2,1,0:T(8,128)(2,1)}, u32[]{:S(2)}, u32[]{:S(2)}) collective-permute-start(bf16[16,7,16,256]{3,2,1,0:T(8,128)(2,1)} %slice.822), channel_id=1, source_target_pairs={{0,1},{1,0},{2,3},{3,2},{4,5},{5,4},{6,7},{7,6},{8,9},{9,8},{10,11... | collective-permute-start | bytes 2752520 | tf_op jit(solution)/shard_map/ppermute | solution.py:22
  109.7 8.0 %all-to-all-start = ((bf16[8,2,512]{2,1,0:T(2,128)(2,1)}), bf16[8,2,512]{2,1,0:T(2,128)(2,1)S(1)}, u32[]{:S(2)}, u32[]{:S(2)}) async-start(bf16[8,2,512]{2,1,0:T(2,128)(2,1)} %reshape.565), calls=%async_computation | async-start | bytes 32768 | tf_op jit(solution)/shard_map/all_to_all | solution.py:156
  140.3 12.7 %collective-permute-start.58 = (f32[2,4,512]{2,0,1:T(2,128)S(1)}, f32[2,4,512]{2,0,1:T(2,128)S(1)}, u32[]{:S(2)}, u32[]{:S(2)}) collective-permute-start(f32[2,4,512]{2,0,1:T(2,128)S(1)} %fusion.200), channel_id=1, source_target_pairs={{0,4},{1,5},{2,6},{3,7},{4,0},{5,1},{6,2},{7,3},{8,12},{9,13},{10,... | collective-permute-start | bytes 49160 | tf_op jit(solution)/shard_map/ppermute | solution.py:22
  148.1 73.8 %collective-permute-start.15 = (bf16[16,512]{1,0:T(8,128)(2,1)S(1)}, bf16[16,512]{1,0:T(8,128)(2,1)}, u32[]{:S(2)}, u32[]{:S(2)}) collective-permute-start(bf16[16,512]{1,0:T(8,128)(2,1)S(1)} %slice.764), channel_id=1, source_target_pairs={{0,16},{8,24},{16,0},{24,8},{1,17},{9,25},{17,1},{25,9},{2,18},{10... | collective-permute-start | bytes 49160 | tf_op jit(solution)/shard_map/ppermute | solution.py:17
  149.8 71.0 %collective-permute-start.11 = (bf16[112,512]{1,0:T(8,128)(2,1)}, bf16[112,512]{1,0:T(8,128)(2,1)}, u32[]{:S(2)}, u32[]{:S(2)}) collective-permute-start(bf16[112,512]{1,0:T(8,128)(2,1)} %get-tuple-element.184), channel_id=1, source_target_pairs={{0,24},{8,0},{16,8},{24,16},{1,25},{9,1},{17,9},{25,17},{2,26},{10... | collective-permute-start | bytes 344072 | tf_op jit(solution)/shard_map/ppermute | solution.py:17
  153.1 9.4 %collective-permute-start.59 = (f32[2,4,512]{2,0,1:T(2,128)S(1)}, f32[2,4,512]{2,0,1:T(2,128)S(1)}, u32[]{:S(2)}, u32[]{:S(2)}) collective-permute-start(f32[2,4,512]{2,0,1:T(2,128)S(1)} %add.795), channel_id=1, source_target_pairs={{0,8},{8,0},{16,24},{24,16},{1,9},{9,1},{17,25},{25,17},{2,10},{10... | collective-permute-start | bytes 49160 | tf_op jit(solution)/shard_map/ppermute | solution.py:22
  155.8 10.8 %collective-permute-start.37 = (bf16[8,7,16,256]{3,2,1,0:T(8,128)(2,1)}, bf16[8,7,16,256]{3,2,1,0:T(8,128)(2,1)S(1)}, u32[]{:S(2)}, u32[]{:S(2)}) collective-permute-start(bf16[8,7,16,256]{3,2,1,0:T(8,128)(2,1)} %get-tuple-element.153), channel_id=1, source_target_pairs={{0,2},{1,3},{2,0},{3,1},{4,6},{5,7},{6,4},{7,5},{8,10},{9,11},{10,... | collective-permute-start | bytes 1376264 | tf_op jit(solution)/shard_map/ppermute | solution.py:22
  159.0 13.2 %collective-permute-start.47 = (bf16[8,7,16,256]{3,2,1,0:T(8,128)(2,1)}, bf16[8,7,16,256]{3,2,1,0:T(8,128)(2,1)S(1)}, u32[]{:S(2)}, u32[]{:S(2)}) collective-permute-start(bf16[8,7,16,256]{3,2,1,0:T(8,128)(2,1)} %get-tuple-element.155), channel_id=1, source_target_pairs={{0,4},{1,5},{2,6},{3,7},{4,0},{5,1},{6,2},{7,3},{8,12},{9,13},{10,... | collective-permute-start | bytes 1376264 | tf_op jit(solution)/shard_map/ppermute | solution.py:22
  162.4 58.4 %collective-permute-start.12 = (bf16[112,512]{1,0:T(8,128)(2,1)}, bf16[112,512]{1,0:T(8,128)(2,1)S(1)}, u32[]{:S(2)}, u32[]{:S(2)}) collective-permute-start(bf16[112,512]{1,0:T(8,128)(2,1)} %get-tuple-element.185), channel_id=1, source_target_pairs={{0,8},{8,16},{16,24},{24,0},{1,9},{9,17},{17,25},{25,1},{2,10},{10... | collective-permute-start | bytes 344072 | tf_op jit(solution)/shard_map/ppermute | solution.py:17
  166.7 7.9 %collective-permute-start.38 = (bf16[4,7,16,256]{3,2,1,0:T(8,128)(2,1)S(1)}, bf16[4,7,16,256]{3,2,1,0:T(8,128)(2,1)S(1)}, u32[]{:S(2)}, u32[]{:S(2)}) collective-permute-start(bf16[4,7,16,256]{3,2,1,0:T(8,128)(2,1)S(1)} %get-tuple-element.161), channel_id=1, source_target_pairs={{0,4},{1,5},{2,6},{3,7},{4,0},{5,1},{6,2},{7,3},{8,12},{9,13},{10,... | collective-permute-start | bytes 688136 | tf_op jit(solution)/shard_map/ppermute | solution.py:22
  172.3 6.1 %collective-permute-start.48 = (bf16[4,7,16,256]{3,2,1,0:T(8,128)(2,1)S(1)}, bf16[4,7,16,256]{3,2,1,0:T(8,128)(2,1)S(1)}, u32[]{:S(2)}, u32[]{:S(2)}) collective-permute-start(bf16[4,7,16,256]{3,2,1,0:T(8,128)(2,1)S(1)} %get-tuple-element.163), channel_id=1, source_target_pairs={{0,2},{1,3},{2,0},{3,1},{4,6},{5,7},{6,4},{7,5},{8,10},{9,11},{10,... | collective-permute-start | bytes 688136 | tf_op jit(solution)/shard_map/ppermute | solution.py:22
  174.7 5.5 %collective-permute-start.39 = (bf16[2,7,16,256]{3,2,1,0:T(8,128)(2,1)S(1)}, bf16[2,7,16,256]{3,2,1,0:T(8,128)(2,1)S(1)}, u32[]{:S(2)}, u32[]{:S(2)}) collective-permute-start(bf16[2,7,16,256]{3,2,1,0:T(8,128)(2,1)S(1)} %get-tuple-element.171), channel_id=1, source_target_pairs={{0,8},{8,0},{16,24},{24,16},{1,9},{9,1},{17,25},{25,17},{2,10},{10... | collective-permute-start | bytes 344072 | tf_op jit(solution)/shard_map/ppermute | solution.py:22
  180.2 7.3 %collective-permute-start.40 = (bf16[1,7,16,256]{3,2,1,0:T(8,128)(2,1)S(1)}, bf16[1,7,16,256]{3,2,1,0:T(8,128)(2,1)S(1)}, u32[]{:S(2)}, u32[]{:S(2)}) collective-permute-start(bf16[1,7,16,256]{3,2,1,0:T(8,128)(2,1)S(1)} %add_convert_fusion.31), channel_id=1, source_target_pairs={{0,16},{8,24},{16,0},{24,8},{1,17},{9,25},{17,1},{25,9},{2,18},{10... | collective-permute-start | bytes 172040 | tf_op jit(solution)/shard_map/ppermute | solution.py:22
  194.3 5.9 %collective-permute-start.52 = (bf16[2,7,16,256]{3,2,1,0:T(8,128)(2,1)S(1)}, bf16[2,7,16,256]{3,2,1,0:T(8,128)(2,1)S(1)}, u32[]{:S(2)}, u32[]{:S(2)}) collective-permute-start(bf16[2,7,16,256]{3,2,1,0:T(8,128)(2,1)S(1)} %pad_maximum_fusion.24), channel_id=1, source_target_pairs={{0,8},{8,0},{16,24},{24,16},{1,9},{9,1},{17,25},{25,17},{2,10},{10... | collective-permute-start | bytes 344072 | tf_op jit(solution)/shard_map/ppermute | solution.py:22
  198.4 8.5 %collective-permute-start.43 = (bf16[4,7,16,256]{3,2,1,0:T(8,128)(2,1)S(1)}, bf16[4,7,16,256]{3,2,1,0:T(8,128)(2,1)S(1)}, u32[]{:S(2)}, u32[]{:S(2)}) collective-permute-start(bf16[4,7,16,256]{3,2,1,0:T(8,128)(2,1)S(1)} %pad_maximum_fusion.15), channel_id=1, source_target_pairs={{0,4},{1,5},{2,6},{3,7},{4,0},{5,1},{6,2},{7,3},{8,12},{9,13},{10,... | collective-permute-start | bytes 688136 | tf_op jit(solution)/shard_map/ppermute | solution.py:22
  200.2 7.7 %collective-permute-start.53 = (bf16[4,7,16,256]{3,2,1,0:T(8,128)(2,1)S(1)}, bf16[4,7,16,256]{3,2,1,0:T(8,128)(2,1)S(1)}, u32[]{:S(2)}, u32[]{:S(2)}) collective-permute-start(bf16[4,7,16,256]{3,2,1,0:T(8,128)(2,1)S(1)} %pad_maximum_fusion.16), channel_id=1, source_target_pairs={{0,2},{1,3},{2,0},{3,1},{4,6},{5,7},{6,4},{7,5},{8,10},{9,11},{10,... | collective-permute-start | bytes 688136 | tf_op jit(solution)/shard_map/ppermute | solution.py:22
  207.0 8.5 %collective-permute-start.44 = (bf16[8,7,16,256]{3,2,1,0:T(8,128)(2,1)S(1)}, bf16[8,7,16,256]{3,2,1,0:T(8,128)(2,1)S(1)}, u32[]{:S(2)}, u32[]{:S(2)}) collective-permute-start(bf16[8,7,16,256]{3,2,1,0:T(8,128)(2,1)S(1)} %pad_maximum_fusion.11), channel_id=1, source_target_pairs={{0,2},{1,3},{2,0},{3,1},{4,6},{5,7},{6,4},{7,5},{8,10},{9,11},{10,... | collective-permute-start | bytes 1376264 | tf_op jit(solution)/shard_map/ppermute | solution.py:22
  208.0 9.1 %collective-permute-start.54 = (bf16[8,7,16,256]{3,2,1,0:T(8,128)(2,1)S(1)}, bf16[8,7,16,256]{3,2,1,0:T(8,128)(2,1)S(1)}, u32[]{:S(2)}, u32[]{:S(2)}) collective-permute-start(bf16[8,7,16,256]{3,2,1,0:T(8,128)(2,1)S(1)} %pad_maximum_fusion.12), channel_id=1, source_target_pairs={{0,4},{1,5},{2,6},{3,7},{4,0},{5,1},{6,2},{7,3},{8,12},{9,13},{10,... | collective-permute-start | bytes 1376264 | tf_op jit(solution)/shard_map/ppermute | solution.py:22
  217.1 9.7 %collective-permute-start.45 = (bf16[16,7,16,256]{3,2,1,0:T(8,128)(2,1)}, bf16[16,7,16,256]{3,2,1,0:T(8,128)(2,1)S(1)}, u32[]{:S(2)}, u32[]{:S(2)}) collective-permute-start(bf16[16,7,16,256]{3,2,1,0:T(8,128)(2,1)} %get-tuple-element.168), channel_id=1, source_target_pairs={{0,1},{1,0},{2,3},{3,2},{4,5},{5,4},{6,7},{7,6},{8,9},{9,8},{10,11... | collective-permute-start | bytes 2752520 | tf_op jit(solution)/shard_map/ppermute | solution.py:22
  220.2 8.7 %collective-permute-start.55 = (bf16[16,7,16,256]{3,2,1,0:T(8,128)(2,1)}, bf16[16,7,16,256]{3,2,1,0:T(8,128)(2,1)}, u32[]{:S(2)}, u32[]{:S(2)}) collective-permute-start(bf16[16,7,16,256]{3,2,1,0:T(8,128)(2,1)} %get-tuple-element.172), channel_id=1, source_target_pairs={{0,1},{1,0},{2,3},{3,2},{4,5},{5,4},{6,7},{7,6},{8,9},{9,8},{10,11... | collective-permute-start | bytes 2752520 | tf_op jit(solution)/shard_map/ppermute | solution.py:22
  223.2 22.2 %all-to-all-start.1 = ((bf16[8,2,512]{2,1,0:T(2,128)(2,1)}), bf16[8,2,512]{2,1,0:T(2,128)(2,1)S(1)}, u32[]{:S(2)}, u32[]{:S(2)}) async-start(bf16[8,2,512]{2,1,0:T(2,128)(2,1)} %reshape.570), calls=%async_computation.1 | async-start | bytes 32768 | tf_op jit(solution)/shard_map/all_to_all | solution.py:156
  239.1 7.9 %collective-permute-start.16 = (bf16[16,7,16,256]{3,2,1,0:T(8,128)(2,1)}, bf16[16,7,16,256]{3,2,1,0:T(8,128)(2,1)}, u32[]{:S(2)}, u32[]{:S(2)}) collective-permute-start(bf16[16,7,16,256]{3,2,1,0:T(8,128)(2,1)} %slice.768), channel_id=1, source_target_pairs={{0,1},{1,0},{2,3},{3,2},{4,5},{5,4},{6,7},{7,6},{8,9},{9,8},{10,11... | collective-permute-start | bytes 2752520 | tf_op jit(solution)/shard_map/ppermute | solution.py:22
  242.2 7.2 %collective-permute-start.26 = (bf16[16,7,16,256]{3,2,1,0:T(8,128)(2,1)S(1)}, bf16[16,7,16,256]{3,2,1,0:T(8,128)(2,1)}, u32[]{:S(2)}, u32[]{:S(2)}) collective-permute-start(bf16[16,7,16,256]{3,2,1,0:T(8,128)(2,1)S(1)} %slice.786), channel_id=1, source_target_pairs={{0,1},{1,0},{2,3},{3,2},{4,5},{5,4},{6,7},{7,6},{8,9},{9,8},{10,11... | collective-permute-start | bytes 2752520 | tf_op jit(solution)/shard_map/ppermute | solution.py:22
  248.6 12.9 %collective-permute-start.17 = (bf16[8,7,16,256]{3,2,1,0:T(8,128)(2,1)S(1)}, bf16[8,7,16,256]{3,2,1,0:T(8,128)(2,1)S(1)}, u32[]{:S(2)}, u32[]{:S(2)}) collective-permute-start(bf16[8,7,16,256]{3,2,1,0:T(8,128)(2,1)S(1)} %get-tuple-element.157), channel_id=1, source_target_pairs={{0,2},{1,3},{2,0},{3,1},{4,6},{5,7},{6,4},{7,5},{8,10},{9,11},{10,... | collective-permute-start | bytes 1376264 | tf_op jit(solution)/shard_map/ppermute | solution.py:22
  250.8 12.8 %collective-permute-start.27 = (bf16[8,7,16,256]{3,2,1,0:T(8,128)(2,1)S(1)}, bf16[8,7,16,256]{3,2,1,0:T(8,128)(2,1)S(1)}, u32[]{:S(2)}, u32[]{:S(2)}) collective-permute-start(bf16[8,7,16,256]{3,2,1,0:T(8,128)(2,1)S(1)} %get-tuple-element.159), channel_id=1, source_target_pairs={{0,4},{1,5},{2,6},{3,7},{4,0},{5,1},{6,2},{7,3},{8,12},{9,13},{10,... | collective-permute-start | bytes 1376264 | tf_op jit(solution)/shard_map/ppermute | solution.py:22
  261.7 8.2 %collective-permute-start.18 = (bf16[4,7,16,256]{3,2,1,0:T(8,128)(2,1)S(1)}, bf16[4,7,16,256]{3,2,1,0:T(8,128)(2,1)S(1)}, u32[]{:S(2)}, u32[]{:S(2)}) collective-permute-start(bf16[4,7,16,256]{3,2,1,0:T(8,128)(2,1)S(1)} %get-tuple-element.165), channel_id=1, source_target_pairs={{0,4},{1,5},{2,6},{3,7},{4,0},{5,1},{6,2},{7,3},{8,12},{9,13},{10,... | collective-permute-start | bytes 688136 | tf_op jit(solution)/shard_map/ppermute | solution.py:22
  263.7 8.1 %collective-permute-start.28 = (bf16[4,7,16,256]{3,2,1,0:T(8,128)(2,1)S(1)}, bf16[4,7,16,256]{3,2,1,0:T(8,128)(2,1)S(1)}, u32[]{:S(2)}, u32[]{:S(2)}) collective-permute-start(bf16[4,7,16,256]{3,2,1,0:T(8,128)(2,1)S(1)} %get-tuple-element.167), channel_id=1, source_target_pairs={{0,2},{1,3},{2,0},{3,1},{4,6},{5,7},{6,4},{7,5},{8,10},{9,11},{10,... | collective-permute-start | bytes 688136 | tf_op jit(solution)/shard_map/ppermute | solution.py:22
  270.0 5.6 %collective-permute-start.19 = (bf16[2,7,16,256]{3,2,1,0:T(8,128)(2,1)S(1)}, bf16[2,7,16,256]{3,2,1,0:T(8,128)(2,1)S(1)}, u32[]{:S(2)}, u32[]{:S(2)}) collective-permute-start(bf16[2,7,16,256]{3,2,1,0:T(8,128)(2,1)S(1)} %get-tuple-element.179), channel_id=1, source_target_pairs={{0,8},{8,0},{16,24},{24,16},{1,9},{9,1},{17,25},{25,17},{2,10},{10... | collective-permute-start | bytes 344072 | tf_op jit(solution)/shard_map/ppermute | solution.py:22
  271.9 5.5 %collective-permute-start.29 = (bf16[2,7,16,256]{3,2,1,0:T(8,128)(2,1)S(1)}, bf16[2,7,16,256]{3,2,1,0:T(8,128)(2,1)S(1)}, u32[]{:S(2)}, u32[]{:S(2)}) collective-permute-start(bf16[2,7,16,256]{3,2,1,0:T(8,128)(2,1)S(1)} %get-tuple-element.183), channel_id=1, source_target_pairs={{0,8},{8,0},{16,24},{24,16},{1,9},{9,1},{17,25},{25,17},{2,10},{10... | collective-permute-start | bytes 344072 | tf_op jit(solution)/shard_map/ppermute | solution.py:22
  275.6 7.9 %collective-permute-start.20 = (bf16[1,7,16,256]{3,2,1,0:T(8,128)(2,1)S(1)}, bf16[1,7,16,256]{3,2,1,0:T(8,128)(2,1)S(1)}, u32[]{:S(2)}, u32[]{:S(2)}) collective-permute-start(bf16[1,7,16,256]{3,2,1,0:T(8,128)(2,1)S(1)} %add_convert_fusion.37), channel_id=1, source_target_pairs={{0,16},{8,24},{16,0},{24,8},{1,17},{9,25},{17,1},{25,9},{2,18},{10... | collective-permute-start | bytes 172040 | tf_op jit(solution)/shard_map/ppermute | solution.py:22
  277.4 7.4 %collective-permute-start.30 = (bf16[1,7,16,256]{3,2,1,0:T(8,128)(2,1)S(1)}, bf16[1,7,16,256]{3,2,1,0:T(8,128)(2,1)S(1)}, u32[]{:S(2)}, u32[]{:S(2)}) collective-permute-start(bf16[1,7,16,256]{3,2,1,0:T(8,128)(2,1)S(1)} %add_convert_fusion.34), channel_id=1, source_target_pairs={{0,16},{8,24},{16,0},{24,8},{1,17},{9,25},{17,1},{25,9},{2,18},{10... | collective-permute-start | bytes 172040 | tf_op jit(solution)/shard_map/ppermute | solution.py:22
  283.6 6.1 %collective-permute-start.21 = (bf16[1,7,16,256]{3,2,1,0:T(8,128)(2,1)S(1)}, bf16[1,7,16,256]{3,2,1,0:T(8,128)(2,1)S(1)}, u32[]{:S(2)}, u32[]{:S(2)}) collective-permute-start(bf16[1,7,16,256]{3,2,1,0:T(8,128)(2,1)S(1)} %get-tuple-element.135), channel_id=1, source_target_pairs={{0,16},{8,24},{16,0},{24,8},{1,17},{9,25},{17,1},{25,9},{2,18},{10... | collective-permute-start | bytes 172040 | tf_op jit(solution)/shard_map/ppermute | solution.py:22
  290.5 5.6 %collective-permute-start.32 = (bf16[2,7,16,256]{3,2,1,0:T(8,128)(2,1)S(1)}, bf16[2,7,16,256]{3,2,1,0:T(8,128)(2,1)S(1)}, u32[]{:S(2)}, u32[]{:S(2)}) collective-permute-start(bf16[2,7,16,256]{3,2,1,0:T(8,128)(2,1)S(1)} %pad_maximum_fusion.22), channel_id=1, source_target_pairs={{0,8},{8,0},{16,24},{24,16},{1,9},{9,1},{17,25},{25,17},{2,10},{10... | collective-permute-start | bytes 344072 | tf_op jit(solution)/shard_map/ppermute | solution.py:22
  294.9 6.1 %collective-permute-start.23 = (bf16[4,7,16,256]{3,2,1,0:T(8,128)(2,1)S(1)}, bf16[4,7,16,256]{3,2,1,0:T(8,128)(2,1)S(1)}, u32[]{:S(2)}, u32[]{:S(2)}) collective-permute-start(bf16[4,7,16,256]{3,2,1,0:T(8,128)(2,1)S(1)} %pad_maximum_fusion.13), channel_id=1, source_target_pairs={{0,4},{1,5},{2,6},{3,7},{4,0},{5,1},{6,2},{7,3},{8,12},{9,13},{10,... | collective-permute-start | bytes 688136 | tf_op jit(solution)/shard_map/ppermute | solution.py:22
  296.1 8.5 %collective-permute-start.33 = (bf16[4,7,16,256]{3,2,1,0:T(8,128)(2,1)S(1)}, bf16[4,7,16,256]{3,2,1,0:T(8,128)(2,1)S(1)}, u32[]{:S(2)}, u32[]{:S(2)}) collective-permute-start(bf16[4,7,16,256]{3,2,1,0:T(8,128)(2,1)S(1)} %pad_maximum_fusion.14), channel_id=1, source_target_pairs={{0,2},{1,3},{2,0},{3,1},{4,6},{5,7},{6,4},{7,5},{8,10},{9,11},{10,... | collective-permute-start | bytes 688136 | tf_op jit(solution)/shard_map/ppermute | solution.py:22
  301.0 10.4 %collective-permute-start.24 = (bf16[8,7,16,256]{3,2,1,0:T(8,128)(2,1)S(1)}, bf16[8,7,16,256]{3,2,1,0:T(8,128)(2,1)S(1)}, u32[]{:S(2)}, u32[]{:S(2)}) collective-permute-start(bf16[8,7,16,256]{3,2,1,0:T(8,128)(2,1)S(1)} %pad_maximum_fusion.9), channel_id=1, source_target_pairs={{0,2},{1,3},{2,0},{3,1},{4,6},{5,7},{6,4},{7,5},{8,10},{9,11},{10,... | collective-permute-start | bytes 1376264 | tf_op jit(solution)/shard_map/ppermute | solution.py:22
  304.7 9.1 %collective-permute-start.34 = (bf16[8,7,16,256]{3,2,1,0:T(8,128)(2,1)S(1)}, bf16[8,7,16,256]{3,2,1,0:T(8,128)(2,1)S(1)}, u32[]{:S(2)}, u32[]{:S(2)}) collective-permute-start(bf16[8,7,16,256]{3,2,1,0:T(8,128)(2,1)S(1)} %pad_maximum_fusion.10), channel_id=1, source_target_pairs={{0,4},{1,5},{2,6},{3,7},{4,0},{5,1},{6,2},{7,3},{8,12},{9,13},{10,... | collective-permute-start | bytes 1376264 | tf_op jit(solution)/shard_map/ppermute | solution.py:22
  312.3 9.8 %collective-permute-start.25 = (bf16[16,7,16,256]{3,2,1,0:T(8,128)(2,1)S(1)}, bf16[16,7,16,256]{3,2,1,0:T(8,128)(2,1)S(1)}, u32[]{:S(2)}, u32[]{:S(2)}) collective-permute-start(bf16[16,7,16,256]{3,2,1,0:T(8,128)(2,1)S(1)} %get-tuple-element.176), channel_id=1, source_target_pairs={{0,1},{1,0},{2,3},{3,2},{4,5},{5,4},{6,7},{7,6},{8,9},{9,8},{10,11... | collective-permute-start | bytes 2752520 | tf_op jit(solution)/shard_map/ppermute | solution.py:22
  314.8 12.0 %collective-permute-start.35 = (bf16[16,7,16,256]{3,2,1,0:T(8,128)(2,1)}, bf16[16,7,16,256]{3,2,1,0:T(8,128)(2,1)S(1)}, u32[]{:S(2)}, u32[]{:S(2)}) collective-permute-start(bf16[16,7,16,256]{3,2,1,0:T(8,128)(2,1)} %get-tuple-element.180), channel_id=1, source_target_pairs={{0,1},{1,0},{2,3},{3,2},{4,5},{5,4},{6,7},{7,6},{8,9},{9,8},{10,11... | collective-permute-start | bytes 2752520 | tf_op jit(solution)/shard_map/ppermute | solution.py:22
  (100 other events, 503.1 us)

commit v2 on v1

v2 whole, which is shorter than its diff:
```python
import functools
import math

import jax
import jax.numpy as jnp
from jax import lax
from jax.experimental import pallas as pl
from jax.experimental.pallas import tpu as pltpu
from jax.sharding import PartitionSpec as P

CO = 2
PIECES = 32
BLOCK = 256
VMEM = pltpu.VMEM
EPSILON = 1e-05
F32 = jnp.float32
BF16 = jnp.bfloat16


def moved(value, axis, by):
    count = lax.axis_size(axis)
    return lax.ppermute(value, axis, [(i, (i + by) % count) for i in range(count)])


def swapped(value, stage):
    axis, bit = stage
    return lax.ppermute(value, axis, [(i, i ^ bit) for i in range(lax.axis_size(axis))])


def axis_bits(axis):
    return [(axis, 1 << k) for k in range(lax.axis_size(axis).bit_length() - 1)]


def added(first, second):
    return (first.astype(F32) + second.astype(F32)).astype(BF16)


def scatter_sum(pieces, order):
    half = pieces.shape[0] // 2
    keep, send = pieces[:half], pieces[half:]
    for step, stage in enumerate(order):
        recv = swapped(send, stage)
        if half == 1:
            return added(keep, recv)
        half //= 2
        send = added(keep[half:], recv[half:])
        keep = added(keep[:half], recv[:half])


def gathered(piece, order):
    for stage in reversed(order):
        piece = jnp.concatenate([piece, swapped(piece, stage)], axis=0)
    return piece


def stage_orders():
    sector, band = axis_bits("sector"), axis_bits("band")
    depth = PIECES.bit_length() - 1
    first = sector + band
    second = sector[:1] + sector[1:][::-1] + band
    return (first[:depth], second[:depth]), first[depth:]


def summed_pieces(pieces):
    orders, rest = stage_orders()
    outs = []
    for part, order in enumerate(orders):
        own = scatter_sum(pieces[part], order)
        for stage in rest:
            own = added(own, swapped(own, stage))
        outs.append(gathered(own, order))
    return outs


def piece_masks():
    orders, _ = stage_orders()
    masks = []
    for order in orders:
        mask, span = 0, PIECES
        for axis, bit in order:
            span //= 2
            mask = mask + ((lax.axis_index(axis) // bit) % 2) * span
        masks.append(mask)
    return masks


def whole():
    return pl.BlockSpec(memory_space=VMEM)


def layer(array, step):
    shape = array.shape[1:]
    return pl.BlockSpec((None,) + shape, lambda *_: (step,) + (0,) * len(shape))


def dot(first, second):
    return jnp.dot(first, second, preferred_element_type=F32)


def dot_rows(first, second):
    return lax.dot_general(first, second, (((0,), (0,)), ((), ())), preferred_element_type=F32)


def dot_columns(first, second):
    return lax.dot_general(first, second, (((1,), (1,)), ((), ())), preferred_element_type=F32)


def split(value):
    high = value.astype(BF16)
    return high, (value - high.astype(F32)).astype(BF16)


def ones_at(equal):
    return jnp.where(equal, 1.0, 0.0).astype(BF16)


def iota(shape, dim):
    return lax.broadcasted_iota(jnp.int32, shape, dim)


def quotient(value, divisor, limit):
    factor = -(-(1 << 18) // divisor)
    assert all((v * factor) >> 18 == v // divisor for v in range(limit))
    return (value * factor) >> 18


def index_kernel(lat, lon, payload, bands, sectors, senders, receivers, send_row, send_col, recv_col):
    own_rows, rim, width = lat * lon, lat * lat, lon + 2 * lat
    ext = 3 * lat * width
    limit = ext + CO * bands * sectors
    value = senders[...]
    row = quotient(value, width, limit)
    col = value - row * width
    block = quotient(row, lat, limit)
    row = row - block * lat
    base = jnp.where(block == 1, 0, jnp.where(block == 0, payload, 2 * payload))
    inside = jnp.where(
        col < lat,
        own_rows + row * lat + col,
        jnp.where(col < lat + lon, row * lon + col - lat, own_rows + rim + row * lat + col - lat - lon),
    )
    coarse = jnp.maximum(value - ext, 0)
    spots = sectors * CO
    band = quotient(coarse, spots, limit)
    spot = coarse - band * spots
    away = band - lax.axis_index("band")
    away = jnp.where(away < 0, away + bands, away)
    head = own_rows + 2 * rim
    coarse_row = jnp.where(
        away == 0,
        head + spot,
        jnp.where(
            away == bands - 1,
            payload + head + spot,
            jnp.where(away == 1, 2 * payload + head + spot, 3 * payload + (away - 2) * spots + spot),
        ),
    )
    result = jnp.where(value < ext, base + inside, coarse_row)
    send_row[...] = result
    slots = value.shape[1]
    send_col[...] = jnp.transpose(jnp.broadcast_to(result, (8, slots)))[:, :1]
    recv_col[...] = jnp.transpose(jnp.broadcast_to(receivers[...], (8, slots)))[:, :1]


def fill_table(table, parts):
    start = 0
    for part in parts:
        table[pl.ds(start, part.shape[0]), :] = part[...]
        start += part.shape[0]
    if start < table.shape[0]:
        table[pl.ds(start, table.shape[0] - start), :] = jnp.zeros(
            (table.shape[0] - start, table.shape[1]), BF16
        )


def activated(pre):
    sigmoid = jax.nn.sigmoid(pre)
    return sigmoid, (pre * sigmoid).astype(BF16)


def normalised(mixed):
    centered = mixed - jnp.mean(mixed, axis=-1, keepdims=True)
    inv_std = lax.rsqrt(jnp.mean(centered * centered, axis=-1, keepdims=True) + EPSILON)
    return centered * inv_std, inv_std


def forward_kernel(parts, own_rows, last, *refs):
    count, send_col, recv_col, recv_row, edges = refs[:5]
    table_parts = refs[5 : 5 + parts]
    w1, c1, w2, g1, v1, d1, v2, g2 = refs[5 + parts : 13 + parts]
    outs = refs[13 + parts : -2]
    table, total = refs[-2:]
    pre_out, norm_out, std_out, node_pre, node_norm, node_std, agg_out, state_out = outs[:8]
    width = w2.shape[1]
    block = pl.program_id(0)

    @pl.when(block == 0)
    def _():
        fill_table(table, table_parts)
        total[...] = jnp.zeros_like(total)

    state = table[pl.ds(0, own_rows), :]
    edge = edges[...]
    rows = edge.shape[0]
    sent = dot(ones_at(iota((rows, table.shape[0]), 1) == send_col[...]), table[...]).astype(BF16)
    received = dot(ones_at(iota((rows, own_rows), 1) == recv_col[...]), state).astype(BF16)
    pre = (
        dot(edge, w1[pl.ds(0, width), :])
        + dot(sent, w1[pl.ds(width, width), :])
        + dot(received, w1[pl.ds(2 * width, width), :])
        + c1[...]
    )
    _, act = activated(pre)
    normed, inv_std = normalised(dot(act, w2[...]))
    live = (iota((rows, 1), 0) + block * rows < count[0]).astype(F32)
    update = normed * g1[...] * live
    pre_out[...] = pre
    norm_out[...] = normed
    std_out[...] = inv_std
    high, low = split(update)
    reach = ones_at(iota((own_rows, rows), 0) == recv_row[...])
    total[...] += dot(reach, high) + dot(reach, low)
    if not last:
        outs[8][...] = (edge.astype(F32) + update).astype(BF16)

    @pl.when(block == pl.num_programs(0) - 1)
    def _():
        agg = total[...].astype(BF16)
        pre = dot(state, v1[pl.ds(0, width), :]) + dot(agg, v1[pl.ds(width, width), :]) + d1[...]
        _, act = activated(pre)
        normed, inv_std = normalised(dot(act, v2[...]))
        node_pre[...] = pre
        node_norm[...] = normed
        node_std[...] = inv_std
        agg_out[...] = agg
        state_out[...] = (state.astype(F32) + normed * g2[...]).astype(BF16)


def mlp_back(grad_out, pre, normed, inv_std, gain, second):
    grad_gain = jnp.sum(grad_out * normed, axis=0, keepdims=True)
    grad_normed = grad_out * gain
    mixed = inv_std * (
        grad_normed
        - jnp.mean(grad_normed, axis=-1, keepdims=True)
        - normed * jnp.mean(grad_normed * normed, axis=-1, keepdims=True)
    )
    mixed = mixed.astype(BF16)
    grad_act = dot_columns(mixed, second)
    sigmoid, act = activated(pre)
    grad_pre = grad_act * sigmoid * (1.0 + pre * (1.0 - sigmoid))
    grad_bias = jnp.sum(grad_pre, axis=0, keepdims=True)
    return act, mixed, grad_pre.astype(BF16), grad_bias, grad_gain


def backward_kernel(own_rows, payload, first, *refs):
    (count, send_row, recv_col, recv_row, grad_state) = refs[:5]
    pre, normed, std, node_pre, node_norm, node_std = refs[5:11]
    w1, w2, g1, v1, v2, g2 = refs[11:17]
    rest = refs[17:]
    if first:
        grad_edges, rest = None, rest
    else:
        grad_edges, rest = rest[0], rest[1:]
    (edge_act, edge_mixed, edge_low, node_act, node_mixed, node_low) = rest[:6]
    (by_sender, by_receiver, near, far, edges_out, vectors) = rest[6:12]
    sums, hubs, spread, bias, gain = rest[12:]
    width = w2.shape[1]
    block = pl.program_id(0)

    @pl.when(block == 0)
    def _():
        act, mixed, low, grad_bias, grad_gain = mlp_back(
            grad_state[...].astype(F32), node_pre[...], node_norm[...], node_std[...], g2[...], v2[...]
        )
        node_act[...], node_mixed[...], node_low[...] = act, mixed, low
        vectors[pl.ds(2, 1), :] = grad_bias
        vectors[pl.ds(3, 1), :] = grad_gain
        spread[...] = dot_columns(low, v1[pl.ds(width, width), :])
        sums[...] = jnp.zeros_like(sums)
        hubs[...] = jnp.zeros_like(hubs)
        bias[...] = jnp.zeros_like(bias)
        gain[...] = jnp.zeros_like(gain)

    rows = pre.shape[0]
    high, low = split(spread[...])
    reach = ones_at(iota((rows, own_rows), 1) == recv_col[...])
    flow = dot(reach, high) + dot(reach, low)
    if not first:
        flow = flow + grad_edges[...]
    flow = flow * (iota((rows, 1), 0) + block * rows < count[0]).astype(F32)
    act, mixed, pre_low, grad_bias, grad_gain = mlp_back(
        flow, pre[...], normed[...], std[...], g1[...], w2[...]
    )
    edge_act[...], edge_mixed[...], edge_low[...] = act, mixed, pre_low
    bias[...] += grad_bias
    gain[...] += grad_gain
    grad = dot_columns(pre_low, w1[pl.ds(0, width), :])
    edges_out[...] = grad if first else grad_edges[...] + grad
    sums[...] += dot(ones_at(iota((sums.shape[0], rows), 0) == send_row[...]), pre_low)
    hubs[...] += dot(ones_at(iota((own_rows, rows), 0) == recv_row[...]), pre_low)

    @pl.when(block == pl.num_programs(0) - 1)
    def _():
        sender_low = sums[...].astype(BF16)
        hub_low = hubs[...].astype(BF16)
        by_sender[...] = sender_low
        by_receiver[...] = hub_low
        table_grad = dot_columns(sender_low, w1[pl.ds(width, width), :])
        own = (
            grad_state[...].astype(F32)
            + dot_columns(node_low[...], v1[pl.ds(0, width), :])
            + dot_columns(hub_low, w1[pl.ds(2 * width, width), :])
        )
        near[pl.ds(0, own_rows), :] = own + table_grad[:own_rows]
        near[pl.ds(own_rows, payload - own_rows), :] = table_grad[own_rows:payload]
        far[...] = table_grad[payload : payload + far.shape[0]].astype(BF16)
        vectors[pl.ds(0, 1), :] = bias[...]
        vectors[pl.ds(1, 1), :] = gain[...]


def weights_kernel(parts, own_rows, *refs):
    edges = refs[0]
    table_parts = refs[1 : 1 + parts]
    (edge_act, edge_mixed, edge_low, node_act, node_mixed, node_low, by_sender, by_receiver, agg) = refs[
        1 + parts : 10 + parts
    ]
    out = refs[10 + parts : 12 + parts]
    table = refs[-1]
    fill_table(table, table_parts)
    masks = piece_masks()
    state = table[pl.ds(0, own_rows), :]
    pairs = [
        (edges[...], edge_low[...]),
        (table[...], by_sender[...]),
        (state, by_receiver[...]),
        (edge_act[...], edge_mixed[...]),
        (state, node_low[...]),
        (agg[...], node_low[...]),
        (node_act[...], node_mixed[...]),
    ]
    for slot, (left, right) in enumerate(pairs):
        grad = dot_rows(left, right).astype(BF16)
        rows, half = grad.shape[0] // PIECES, grad.shape[1] // 2
        for piece in range(PIECES):
            for part in range(2):
                out[part][piece ^ masks[part], slot] = grad[
                    piece * rows : (piece + 1) * rows, part * half : (part + 1) * half
                ]


def results_kernel(step, factor, given, *refs):
    sums = refs[:2]
    vectors = refs[2]
    refs = refs[3 + given :]
    outs, vector_outs = refs[:4], refs[4:-2]
    stage, done = refs[-2:]
    masks = piece_masks()
    width = stage.shape[-1]
    copies = []
    slot = 0
    for out in outs:
        for part in range(out.shape[1] // width):
            rows, half = width // PIECES, width // 2
            for piece in range(PIECES):
                for side in range(2):
                    stage[slot, pl.ds(piece * rows, rows), pl.ds(side * half, half)] = (
                        sums[side][piece ^ masks[side], slot].astype(F32) * factor
                    )
            copy = pltpu.make_async_copy(
                stage.at[slot], out.at[step, pl.ds(part * width, width), :], done.at[slot]
            )
            copy.start()
            copies.append(copy)
            slot += 1
    for item, out in enumerate(vector_outs):
        out[...] = vectors[:, item] * factor
    for copy in copies:
        copy.wait()


def summed_vectors(values):
    for stage in axis_bits("sector") + axis_bits("band"):
        values = values + swapped(values, stage)
    return values


def collected(state, lat, lon):
    width = state.shape[-1]
    grid = state.reshape(lat, lon, width)
    sectors, bands = lax.axis_size("sector"), lax.axis_size("band")
    here = lax.axis_index("sector")
    rims = jnp.concatenate([grid[:, :lat], grid[:, lon - lat :]], axis=1)
    around = lax.all_gather(rims, "sector")
    west = lax.dynamic_index_in_dim(around, (here + sectors - 1) % sectors, 0, False)[:, lat:]
    east = lax.dynamic_index_in_dim(around, (here + 1) % sectors, 0, False)[:, :lat]
    coarse = around[:, 0, :CO].reshape(sectors * CO, width)
    payload = jnp.concatenate(
        [state, west.reshape(lat * lat, width), east.reshape(lat * lat, width), coarse], axis=0
    )
    north = moved(payload, "band", 1)
    south = moved(payload, "band", -1)
    others = [moved(coarse, "band", -away) for away in range(2, bands - 1)]
    return [payload, north, south] + others


def returned(near, low, lat, lon, payload):
    width = near.shape[-1]
    sectors, bands = lax.axis_size("sector"), lax.axis_size("band")
    own_rows, rim = lat * lon, lat * lat
    head = own_rows + 2 * rim
    from_south = moved(low[:payload], "band", -1)
    from_north = moved(low[payload : 2 * payload], "band", 1)
    total = near + from_south.astype(F32) + from_north.astype(F32)
    coarse = total[head:]
    for away in range(2, bands - 1):
        start = 2 * payload + (away - 2) * sectors * CO
        coarse = coarse + moved(low[start : start + sectors * CO], "band", away).astype(F32)
    rims = total[own_rows:head].astype(BF16)
    from_east = moved(rims[:rim], "sector", -1).astype(F32).reshape(lat, lat, width)
    from_west = moved(rims[rim:], "sector", 1).astype(F32).reshape(lat, lat, width)
    spread = lax.all_to_all(
        coarse.astype(BF16).reshape(sectors, CO, width), "sector", 0, 0, tiled=True
    )
    mine = jnp.sum(spread.astype(F32), axis=0)
    grid = total[:own_rows].reshape(lat, lon, width)
    grid = grid.at[:, lon - lat :].add(from_east).at[:, :lat].add(from_west)
    return grid.reshape(own_rows, width).at[:CO].add(mine)


def local(
    node_states,
    edge_states,
    senders,
    receivers,
    edge_count,
    edge_hidden,
    edge_offset,
    edge_output,
    edge_scale,
    node_hidden,
    node_offset,
    node_output,
    node_scale,
    output_cotangent,
):
    lat, lon, width = node_states.shape
    own_rows = lat * lon
    slots = edge_states.shape[1]
    depth = edge_hidden.shape[0]
    sectors, bands = lax.axis_size("sector"), lax.axis_size("band")
    payload = own_rows + 2 * lat * lat + sectors * CO
    table_rows = 3 * payload + (bands - 3) * sectors * CO
    padded = -(-table_rows // 128) * 128
    blocks = slots // BLOCK
    shape = jax.ShapeDtypeStruct
    row_vectors = [v[:, None] for v in (edge_offset, edge_scale, node_offset, node_scale)]
    c1, g1, d1, g2 = row_vectors

    send_row, send_col, recv_col = pl.pallas_call(
        functools.partial(index_kernel, lat, lon, payload, bands, sectors),
        out_shape=(shape((1, slots), jnp.int32), shape((slots, 1), jnp.int32), shape((slots, 1), jnp.int32)),
        name="index",
    )(senders, receivers)

    smem = pl.BlockSpec(memory_space=pltpu.SMEM)
    by_rows = pl.BlockSpec((BLOCK, width), lambda i: (i, 0))
    by_col = pl.BlockSpec((BLOCK, 1), lambda i: (i, 0))
    by_row = pl.BlockSpec((1, BLOCK), lambda i: (0, i))

    def fixed(*dims):
        return pl.BlockSpec(dims, lambda i: (0,) * len(dims))

    unit = slots * width * width * 2
    state = node_states.reshape(own_rows, width)
    edge_rows = edge_states[0]
    records = []
    for step in range(depth):
        last = step == depth - 1
        parts = collected(state, lat, lon)
        out_shape = [
            shape((slots, width), F32),
            shape((slots, width), F32),
            shape((slots, 1), F32),
            shape((own_rows, width), F32),
            shape((own_rows, width), F32),
            shape((own_rows, 1), F32),
            shape((own_rows, width), BF16),
            shape((own_rows, width), BF16),
        ] + ([] if last else [shape((slots, width), BF16)])
        wide, thin = fixed(own_rows, width), fixed(own_rows, 1)
        out_specs = [by_rows, by_rows, by_col, wide, wide, thin, wide, wide] + ([] if last else [by_rows])
        weights = (edge_hidden, c1, edge_output, g1, node_hidden, d1, node_output, g2)
        outs = pl.pallas_call(
            functools.partial(forward_kernel, len(parts), own_rows, last),
            grid=(blocks,),
            out_shape=out_shape,
            in_specs=[smem, by_col, by_col, by_row, by_rows]
            + [fixed(*p.shape) for p in parts]
            + [layer(w, step) for w in weights],
            out_specs=out_specs,
            scratch_shapes=[VMEM((padded, width), BF16), VMEM((own_rows, width), F32)],
            cost_estimate=pl.CostEstimate(flops=6 * unit, bytes_accessed=8 << 20, transcendentals=slots * width),
            name="forward",
        )(edge_count, send_col, recv_col, receivers, edge_rows, *parts, *weights)
        records.append((edge_rows, parts, outs))
        state = outs[7]
        if not last:
            edge_rows = outs[8]
    node_result = state.reshape(lat, lon, width)
    grad_state = output_cotangent.reshape(own_rows, width)
    grad_edges = None
    vectors = [None] * depth
    factor = 1.0 / math.sqrt(own_rows * bands * sectors)
    sums = [None] * depth
    for step in reversed(range(depth)):
        first = grad_edges is None
        edge_rows, parts, outs = records[step]
        pre, normed, std, node_pre, node_norm, node_std, agg = outs[:7]
        wide, thin = fixed(own_rows, width), fixed(own_rows, 1)
        weights = (edge_hidden, edge_output, g1, node_hidden, node_output, g2)
        acts = pl.pallas_call(
            functools.partial(backward_kernel, own_rows, payload, first),
            grid=(blocks,),
            in_specs=[smem, by_row, by_col, by_row, wide, by_rows, by_rows, by_col, wide, wide, thin]
            + [layer(w, step) for w in weights]
            + ([] if first else [by_rows]),
            out_shape=[shape((slots, width), BF16)] * 3
            + [shape((own_rows, width), BF16)] * 3
            + [
                shape((padded, width), BF16),
                shape((own_rows, width), BF16),
                shape((payload, width), F32),
                shape((table_rows - payload, width), BF16),
                shape((slots, width), F32),
                shape((4, width), F32),
            ],
            out_specs=[by_rows] * 3
            + [wide] * 3
            + [
                fixed(padded, width),
                wide,
                fixed(payload, width),
                fixed(table_rows - payload, width),
                by_rows,
                fixed(4, width),
            ],
            scratch_shapes=[
                VMEM((padded, width), F32),
                VMEM((own_rows, width), F32),
                VMEM((own_rows, width), F32),
                VMEM((1, width), F32),
                VMEM((1, width), F32),
            ],
            cost_estimate=pl.CostEstimate(flops=8 * unit, bytes_accessed=10 << 20, transcendentals=slots * width),
            name="backward",
        )(
            edge_count, send_row, recv_col, receivers, grad_state, pre, normed, std, node_pre, node_norm,
            node_std, *weights, *([] if first else [grad_edges])
        )
        grad_edges = acts[10]
        vectors[step] = acts[11]
        grad_state = returned(acts[8], acts[9], lat, lon, payload)
        slots7 = (edge_hidden.shape[1] + edge_output.shape[1] + node_hidden.shape[1] + node_output.shape[1]) // width
        piece = shape((PIECES, slots7, width // PIECES, width // 2), BF16)
        pieces = pl.pallas_call(
            functools.partial(weights_kernel, len(parts), own_rows),
            out_shape=(piece, piece),
            scratch_shapes=[VMEM((padded, width), BF16)],
            cost_estimate=pl.CostEstimate(flops=6 * unit, bytes_accessed=10 << 20, transcendentals=0),
            name="weights",
        )(edge_rows, *parts, *acts[:8], agg)
        sums[step] = summed_pieces(pieces)
    total = summed_vectors(jnp.stack(vectors))
    given = []
    for step in reversed(range(depth)):
        final = step == 0
        anywhere = pl.BlockSpec(memory_space=pl.ANY)
        arrays = (edge_hidden, edge_output, node_hidden, node_output)
        outs = pl.pallas_call(
            functools.partial(results_kernel, step, factor, len(given)),
            in_specs=[whole()] * 3 + [anywhere] * len(given),
            out_shape=[shape(a.shape, F32) for a in arrays] + ([shape((depth, width), F32)] * 4 if final else []),
            out_specs=[anywhere] * 4 + ([whole()] * 4 if final else []),
            input_output_aliases={3 + k: k for k in range(len(given))},
            scratch_shapes=[VMEM((slots7, width, width), F32), pltpu.SemaphoreType.DMA((slots7,))],
            cost_estimate=pl.CostEstimate(flops=1 << 20, bytes_accessed=8 << 20, transcendentals=0),
            name="results",
        )(*sums[step], total if final else vectors[step][None], *given)
        given = list(outs[:4])
    return (
        node_result,
        grad_state.reshape(lat, lon, width),
        grad_edges[None],
        outs[0],
        outs[4],
        outs[1],
        outs[5],
        outs[2],
        outs[6],
        outs[3],
        outs[7],
    )


def solution(mesh):
    grid = P("band", "sector", None)
    edges = P(("band", "sector"), None, None)
    index = P(("band", "sector"), None)
    return jax.shard_map(
        local,
        mesh=mesh,
        in_specs=(grid, edges, index, index, P(("band", "sector"))) + (P(),) * 8 + (grid,),
        out_specs=(grid, grid, edges) + (P(),) * 8,
        check_vma=False,
    )
```

time: 350 us -> 268 us (0.77); the launches traced: 344 us -> 267 us
  Pallas kernels: 0 us -> 53.9 us
  local copies, waits for them, and re-layouts: 85.5 us -> 40.6 us
  matrix products: 33.3 us -> 0 us
  other arithmetic: 47.4 us -> 14.6 us
  waiting for transfers between devices: 80.3 us -> 57.7 us
  starting transfers between devices: 73.6 us -> 77.9 us
    pallas_call x0 -> x9, Pallas kernels: none -> 53.9 us  [the longest x2 16.1 us: local(): pl.pallas_call(functools.partial(backward_kernel, own_rows, payload, firs...]
    dot_general x44 -> x0, matrix products: 33.3 us -> none  [the longest x8 8.08 us: picked(): return out + lax.dot_general(onehot, low, dims, preferred_element_type=F32)]
    ppermute x45, waiting for transfers between devices: 71.3 us -> 40.5 us  [swapped(): lax.ppermute(value, axis, [(i, i ^ bit) for i in range(lax.axis_size(axis...]
    gather x8 -> x0, local copies, waits for them, and re-layouts: 21.7 us -> none  [the longest x4 11.5 us: local(): jnp.take(stacked[..., part * half:(part + 1) * half], index[part], axis=0)]
    unnamed x198 -> x58, local copies, waits for them, and re-layouts: 29.9 us -> 13.7 us
    select_n x7 -> x0, other arithmetic: 10.8 us -> none  [the longest x4 6.59 us: local(): jnp.take(sums[step][part], index[part], axis=0)]
    slice x10 -> x0, local copies, waits for them, and re-layouts: 9.54 us -> none  [the longest x2 4.14 us: local(): stacked[..., part * half:(part + 1) * half]]
    another operation x8 -> x3, other arithmetic: 10.8 us -> 1.73 us  [the longest x3 8.31 us: local(): matrices = jnp.stack(matrices)]
  transfers between devices with their start and end apart: 63 -> 63, of which waited for: 33 -> 23; matrix products, arithmetic and copies ran while one was open for 31% -> 16% of each run, Pallas kernels for 0% -> 6%
where the time goes in v2:
time: 268 us; the launch traced here: 267 us
  starting transfers between devices  77.9 us (29%)
  waiting for transfers between devices  57.7 us (22%)
  Pallas kernels  53.9 us (20%)
  local copies, waits for them, and re-layouts  40.6 us (15%)
  blocking collectives  20.1 us (8%)
  other arithmetic  14.6 us (5%)
    ppermute x45, starting transfers between devices, swapped(): lax.ppermute(value, axis, [(i, i ^ bit) for i in range(lax.axis_size(axis...  48.9 us
    ppermute x45, waiting for transfers between devices, swapped(): lax.ppermute(value, axis, [(i, i ^ bit) for i in range(lax.axis_size(axis...  40.5 us
    ppermute x16, starting transfers between devices, moved(): lax.ppermute(value, axis, [(i, (i + by) % count) for i in range(count)])  22 us
    all_gather x2, blocking collectives, collected(): around = lax.all_gather(rims, 'sector')  20.1 us
    pallas_call x2, Pallas kernels, local(): pl.pallas_call(functools.partial(backward_kernel, own_rows, payload, firs...  16.1 us
    pallas_call x2, Pallas kernels, local(): pl.pallas_call(functools.partial(forward_kernel, len(parts), own_rows, la...  14.7 us
    unnamed x58, local copies, waits for them, and re-layouts  13.7 us
    ppermute x16, waiting for transfers between devices, moved(): lax.ppermute(value, axis, [(i, (i + by) % count) for i in range(count)])  13.3 us
  transfers between devices with their start and end apart: 63, of which 23 were waited for; matrix products, arithmetic and copies ran while one was open for 16% of the time, Pallas kernels for 6%

profile of v2, /device:TPU:0, one launch (start us, length us, event | category | flops | bytes accessed | tf_op | source)
XLA Modules:
  0.0 267.0 jit_solution(4869491354894327589)
XLA Ops:
  1.5 10.8 %all-gather = bf16[32,8,512]{2,1,0:T(8,128)(2,1)S(1)} all-gather(bf16[4,8,512]{2,1,0:T(8,128)(2,1)S(1)} %pad_maximum_fusion.13), channel_id=2, replica_groups=mesh['band'=4,'sector'=8] {'sector'}, dimensions={0}, use_global_device_ids=true | all-gather | bytes 294912 | tf_op jit(solution)/shard_map/all_gather | solution.py:393
  13.3 3.7 %collective-permute-start.1 = (bf16[112,512]{1,0:T(8,128)(2,1)S(1)}, bf16[112,512]{1,0:T(8,128)(2,1)S(1)}, u32[]{:S(2)}, u32[]{:S(2)}) collective-permute-start(bf16[112,512]{1,0:T(8,128)(2,1)S(1)} %pad_maximum_fusion.8.refs_5_.refs_1_), channel_id=1, source_target_pairs={{0,24},{8,0},{16,8},{24,16},{1,25},{9,1},{17,9},{25,17},{2,26},{10... | collective-permute-start | bytes 344072 | tf_op jit(solution)/shard_map/ppermute | solution.py:22
  26.1 7.4 %forward.2 = (f32[512,512]{1,0:T(8,128)}, f32[512,512]{1,0:T(8,128)}, f32[512,1]{1,0:T(8,128)}, f32[64,512]{1,0:T(8,128)}, f32[64,512]{1,0:T(8,128)}, /*index=5*...) custom-call(s32[1]{0:T(128)S(6)} %copy.82.refs_0_, ...), custom_call_target="tpu_custom_call" | custom-call | flops 1610612736 | bytes 8388608 | tf_op jit(solution)/shard_map/forward/pallas_call | solution.py:493
  35.2 9.3 %all-gather.1 = bf16[32,8,512]{2,1,0:T(8,128)(2,1)S(1)} all-gather(bf16[4,8,512]{2,1,0:T(8,128)(2,1)S(1)} %pad_maximum_fusion.14), channel_id=3, replica_groups=mesh['band'=4,'sector'=8] {'sector'}, dimensions={0}, use_global_device_ids=true | all-gather | bytes 294912 | tf_op jit(solution)/shard_map/all_gather | solution.py:393
  44.7 2.9 %collective-permute-start.4 = (bf16[112,512]{1,0:T(8,128)(2,1)S(1)}, bf16[112,512]{1,0:T(8,128)(2,1)S(1)}, u32[]{:S(2)}, u32[]{:S(2)}) collective-permute-start(bf16[112,512]{1,0:T(8,128)(2,1)S(1)} %constant_dynamic-update-slice_fusion.refs_5_.refs_1_), channel_id=1, source_target_pairs={{0,24},{8,0},{16,8},{24,16},{1,25},{9,1},{17,9},{25,17},{2,26},{10... | collective-permute-start | bytes 344072 | tf_op jit(solution)/shard_map/ppermute | solution.py:22
  49.6 6.5 %collective-permute-done.5.refs_8_.refs_4_ = bf16[16,512]{1,0:T(8,128)(2,1)S(1)} collective-permute-done((bf16[16,512]{1,0:T(8,128)(2,1)S(1)}, bf16[16,512]{1,0:T(8,128)(2,1)S(1)}, u32[]{:S(2)}, u32[]{:S(2)}) %collective-permute-start.5) | collective-permute-done | bytes 16416 | tf_op jit(solution)/shard_map/ppermute | solution.py:22
  56.8 7.3 %forward.3 = (f32[512,512]{1,0:T(8,128)}, f32[512,512]{1,0:T(8,128)}, f32[512,1]{1,0:T(8,128)}, f32[64,512]{1,0:T(8,128)}, f32[64,512]{1,0:T(8,128)}, /*index=5*...) custom-call(s32[1]{0:T(128)S(6)} %copy.82.refs_0_, s32[512,1]{1,0:T(8,128)} %get-tuple-element.143.refs_1_, ...), custom_call_target="tpu_custom_call" | custom-call | flops 1610612736 | bytes 8388608 | tf_op jit(solution)/shard_map/forward/pallas_call | solution.py:493
  64.1 8.0 %backward.2 = (bf16[512,512]{1,0:T(8,128)(2,1)}, bf16[512,512]{1,0:T(8,128)(2,1)}, bf16[512,512]{1,0:T(8,128)(2,1)}, bf16[64,512]{1,0:T(8,128)(2,1)}, bf16[64,51...) custom-call(s32[1]{0:T(128)S(6)} %copy.82.refs_0_, ...), custom_call_target="tpu_custom_call" | custom-call | flops 2147483648 | bytes 10485760 | tf_op jit(solution)/shard_map/backward/pallas_call | solution.py:521
  73.0 1.9 collective-permute-start.6
  76.5 1.9 collective-permute-done.6
  78.4 3.3 %collective-permute-done.7 = bf16[112,512]{1,0:T(8,128)(2,1)S(1)} collective-permute-done((bf16[112,512]{1,0:T(8,128)(2,1)S(1)}, bf16[112,512]{1,0:T(8,128)(2,1)S(1)}, u32[]{:S(2)}, u32[]{:S(2)}) %collective-permute-start.7) | collective-permute-done | bytes 114720 | tf_op jit(solution)/shard_map/ppermute | solution.py:22
  83.4 3.3 %all-to-all-start = ((bf16[8,2,512]{2,1,0:T(2,128)(2,1)}), bf16[8,2,512]{2,1,0:T(2,128)(2,1)S(1)}, u32[]{:S(2)}, u32[]{:S(2)}) async-start(bf16[8,2,512]{2,1,0:T(2,128)(2,1)} %reshape.258), calls=%async_computation | async-start | bytes 32768 | tf_op jit(solution)/shard_map/all_to_all | solution.py:421
  87.2 2.3 collective-permute-start.8
  89.4 2.0 all-to-all-done
  92.2 8.2 %backward.3 = (bf16[512,512]{1,0:T(8,128)(2,1)}, bf16[512,512]{1,0:T(8,128)(2,1)}, bf16[512,512]{1,0:T(8,128)(2,1)}, bf16[64,512]{1,0:T(8,128)(2,1)}, bf16[64,51...) custom-call(s32[1]{0:T(128)S(6)} %copy.82.refs_0_, ...), custom_call_target="tpu_custom_call" | custom-call | flops 2147483648 | bytes 10485760 | tf_op jit(solution)/shard_map/backward/pallas_call | solution.py:521
  103.2 2.4 collective-permute-start.37
  105.5 1.7 collective-permute-done.37
  109.1 5.2 %weights.3 = (bf16[32,7,16,256]{3,2,1,0:T(8,128)(2,1)}, bf16[32,7,16,256]{3,2,1,0:T(8,128)(2,1)}) custom-call(bf16[512,512]{1,0:T(8,128)(2,1)} %get-tuple-element.145.refs_4_.refs_0_, bf16[112,512]{1,0:T(8,128)(2,1)} %copy-done.9, bf16[112,512]{1,0:T(8,128)(2,1)} %copy-done.16, bf16[112,512]{1,0:T(8,128)(2,1)} %copy-done.15, bf16[16,512]{1,0:T(8,128)(2,1)} %copy-done.18, ...), custom_call_target="tpu_custom_call" | custom-call | flops 1610612736 | bytes 10485760 | tf_op jit(solution)/shard_map/weights/pallas_call | solution.py:565
  118.5 1.8 collective-permute-start.11
  122.5 5.2 %weights.2 = (bf16[32,7,16,256]{3,2,1,0:T(8,128)(2,1)}, bf16[32,7,16,256]{3,2,1,0:T(8,128)(2,1)}) custom-call(bf16[512,512]{1,0:T(8,128)(2,1)} %bitcast.30, bf16[112,512]{1,0:T(8,128)(2,1)} %copy-done.7, bf16[112,512]{1,0:T(8,128)(2,1)} %copy-done.14, bf16[112,512]{1,0:T(8,128)(2,1)} %copy-done.13, bf16[16,512]{1,0:T(8,128)(2,1)} %copy-done.17, ...), custom_call_target="tpu_custom_call" | custom-call | flops 1610612736 | bytes 10485760 | tf_op jit(solution)/shard_map/weights/pallas_call | solution.py:565
  127.7 2.4 slice.461
  131.1 2.0 collective-permute-start.15
  136.4 3.6 %all-to-all-start.1 = ((bf16[8,2,512]{2,1,0:T(2,128)(2,1)}), bf16[8,2,512]{2,1,0:T(2,128)(2,1)S(1)}, u32[]{:S(2)}, u32[]{:S(2)}) async-start(bf16[8,2,512]{2,1,0:T(2,128)(2,1)} %reshape.263), calls=%async_computation.1 | async-start | bytes 32768 | tf_op jit(solution)/shard_map/all_to_all | solution.py:421
  140.0 2.7 %collective-permute-start.13 = (bf16[16,512]{1,0:T(8,128)(2,1)S(1)}, bf16[16,512]{1,0:T(8,128)(2,1)S(1)}, u32[]{:S(2)}, u32[]{:S(2)}) collective-permute-start(bf16[16,512]{1,0:T(8,128)(2,1)S(1)} %get-tuple-element.272), channel_id=1, source_target_pairs={{0,7},{1,0},{2,1},{3,2},{4,3},{5,4},{6,5},{7,6},{8,15},{9,8},{10,9... | collective-permute-start | bytes 49160 | tf_op jit(solution)/shard_map/ppermute | solution.py:22
  142.7 2.0 all-to-all-done.1
  144.9 1.7 add_convert_fusion.1
  148.7 2.3 collective-permute-start.42
  155.2 4.8 %collective-permute-done.52 = bf16[8,7,16,256]{3,2,1,0:T(8,128)(2,1)S(1)} collective-permute-done((bf16[8,7,16,256]{3,2,1,0:T(8,128)(2,1)S(1)}, bf16[8,7,16,256]{3,2,1,0:T(8,128)(2,1)S(1)}, u32[]{:S(2)}, u32[]{:S(2)}) %collective-permute-start.52) | collective-permute-done | bytes 458784 | tf_op jit(solution)/shard_map/ppermute | solution.py:27
  163.8 6.1 %collective-permute-done.27 = bf16[8,7,16,256]{3,2,1,0:T(8,128)(2,1)S(1)} collective-permute-done((bf16[8,7,16,256]{3,2,1,0:T(8,128)(2,1)S(1)}, bf16[8,7,16,256]{3,2,1,0:T(8,128)(2,1)S(1)}, u32[]{:S(2)}, u32[]{:S(2)}) %collective-permute-start.27) | collective-permute-done | bytes 458784 | tf_op jit(solution)/shard_map/ppermute | solution.py:27
  173.6 3.5 %collective-permute-done.53 = bf16[4,7,16,256]{3,2,1,0:T(8,128)(2,1)S(1)} collective-permute-done((bf16[4,7,16,256]{3,2,1,0:T(8,128)(2,1)S(1)}, bf16[4,7,16,256]{3,2,1,0:T(8,128)(2,1)S(1)}, u32[]{:S(2)}, u32[]{:S(2)}) %collective-permute-start.53) | collective-permute-done | bytes 229408 | tf_op jit(solution)/shard_map/ppermute | solution.py:27
  177.2 2.3 collective-permute-start.54
  179.7 3.6 %collective-permute-done.54 = bf16[2,7,16,256]{3,2,1,0:T(8,128)(2,1)S(1)} collective-permute-done((bf16[2,7,16,256]{3,2,1,0:T(8,128)(2,1)S(1)}, bf16[2,7,16,256]{3,2,1,0:T(8,128)(2,1)S(1)}, u32[]{:S(2)}, u32[]{:S(2)}) %collective-permute-start.54) | collective-permute-done | bytes 114720 | tf_op jit(solution)/shard_map/ppermute | solution.py:27
  183.4 1.9 collective-permute-start.55
  186.6 2.1 collective-permute-start.29
  188.9 2.0 collective-permute-done.45
  195.7 3.2 %collective-permute-done.56 = bf16[1,7,16,256]{3,2,1,0:T(8,128)(2,1)S(1)} collective-permute-done((bf16[1,7,16,256]{3,2,1,0:T(8,128)(2,1)S(1)}, bf16[1,7,16,256]{3,2,1,0:T(8,128)(2,1)S(1)}, u32[]{:S(2)}, u32[]{:S(2)}) %collective-permute-start.56) | collective-permute-done | bytes 57376 | tf_op jit(solution)/shard_map/ppermute | solution.py:27
  202.4 1.9 collective-permute-start.20
  205.5 3.7 %collective-permute-done.20 = bf16[1,7,16,256]{3,2,1,0:T(8,128)(2,1)S(1)} collective-permute-done((bf16[1,7,16,256]{3,2,1,0:T(8,128)(2,1)S(1)}, bf16[1,7,16,256]{3,2,1,0:T(8,128)(2,1)S(1)}, u32[]{:S(2)}, u32[]{:S(2)}) %collective-permute-start.20) | collective-permute-done | bytes 57376 | tf_op jit(solution)/shard_map/ppermute | solution.py:27
  211.4 2.6 collective-permute-start.31
  215.5 1.7 collective-permute-start.48
  218.6 1.9 collective-permute-start.32
  237.0 3.8 %collective-permute-done.49 = bf16[8,7,16,256]{3,2,1,0:T(8,128)(2,1)S(1)} collective-permute-done((bf16[8,7,16,256]{3,2,1,0:T(8,128)(2,1)S(1)}, bf16[8,7,16,256]{3,2,1,0:T(8,128)(2,1)S(1)}, u32[]{:S(2)}, u32[]{:S(2)}) %collective-permute-start.49) | collective-permute-done | bytes 458784 | tf_op jit(solution)/shard_map/ppermute | solution.py:27
  243.2 2.5 collective-permute-done.24
  248.5 2.9 %constant_dynamic-update-slice_fusion.42.refs_1_ = bf16[32,7,16,256]{3,2,1,0:T(8,128)(2,1)} fusion(bf16[32,7,16,256]{3,2,1,0:T(8,128)(2,1)} %get-tuple-element.232, bf16[16,7,16,256]{3,2,1,0:T(8,128)(2,1)} %collective-permute-done.60), kind=kLoop, calls=%fused_computation.93 | loop fusion | bytes 1835008 | tf_op jit(solution)/shard_map/concatenate | solution.py:52
  251.4 5.2 %results.2 = (f32[2,1536,512]{2,1,0:T(8,128)}, f32[2,512,512]{2,1,0:T(8,128)}, f32[2,1024,512]{2,1,0:T(8,128)}, f32[2,512,512]{2,1,0:T(8,128)}) custom-call(bf16[32,7,16,256]{3,2,1,0:T(8,128)(2,1)} %copy-done, bf16[32,7,16,256]{3,2,1,0:T(8,128)(2,1)} %constant_dynamic-update-slice_fusion.42.refs_1_, f32[1,4,512]{2,1,0:T(4,128)} %bitcast.40), custom_call_target="tpu_custom_call" | custom-call | flops 1048576 | bytes 8388608 | tf_op jit(solution)/shard_map/results/pallas_call | solution.py:579
  256.6 2.2 constant_dynamic-update-slice_fusion.9.refs_0_
  258.9 2.2 constant_dynamic-update-slice_fusion.20.refs_1_
  261.0 5.8 %results.3 = (f32[2,1536,512]{2,1,0:T(8,128)}, f32[2,512,512]{2,1,0:T(8,128)}, f32[2,1024,512]{2,1,0:T(8,128)}, f32[2,512,512]{2,1,0:T(8,128)}, f32[2,512]{1,0:T...) custom-call(bf16[32,7,16,256]{3,2,1,0:T(8,128)(2,1)} %constant_dynam, ...), custom_call_target="tpu_custom_call", output_to_operand_aliasing={{0}: (3, {}), {1}: (4, {}), {2}: (5, {}), {3}: (6, {})} | custom-call | flops 1048576 | bytes 8388608 | tf_op jit(solution)/shard_map/results/pallas_call | solution.py:579
  (246 shorter events, 87.0 us)
Async XLA Ops:
  13.3 12.1 %collective-permute-start.1 = (bf16[112,512]{1,0:T(8,128)(2,1)S(1)}, bf16[112,512]{1,0:T(8,128)(2,1)S(1)}, u32[]{:S(2)}, u32[]{:S(2)}) collective-permute-start(bf16[112,512]{1,0:T(8,128)(2,1)S(1)} %pad_maximum_fusion.8.refs_5_.refs_1_), channel_id=1, source_target_pairs={{0,24},{8,0},{16,8},{24,16},{1,25},{9,1},{17,9},{25,17},{2,26},{10... | collective-permute-start | bytes 344072 | tf_op jit(solution)/shard_map/ppermute | solution.py:22
  16.9 8.5 %collective-permute-start = (bf16[112,512]{1,0:T(8,128)(2,1)S(1)}, bf16[112,512]{1,0:T(8,128)(2,1)S(1)}, u32[]{:S(2)}, u32[]{:S(2)}) collective-permute-start(bf16[112,512]{1,0:T(8,128)(2,1)S(1)} %pad_maximum_fusion.8.refs_5_.refs_1_), channel_id=1, source_target_pairs={{0,8},{8,16},{16,24},{24,0},{1,9},{9,17},{17,25},{25,1},{2,10},{10... | collective-permute-start | bytes 344072 | tf_op jit(solution)/shard_map/ppermute | solution.py:22
  16.9 8.5 %collective-permute-start.2 = (bf16[16,512]{1,0:T(8,128)(2,1)S(1)}, bf16[16,512]{1,0:T(8,128)(2,1)S(1)}, u32[]{:S(2)}, u32[]{:S(2)}) collective-permute-start(bf16[16,512]{1,0:T(8,128)(2,1)S(1)} %reshape_squeeze.6), channel_id=1, source_target_pairs={{0,16},{8,24},{16,0},{24,8},{1,17},{9,25},{17,1},{25,9},{2,18},{10... | collective-permute-start | bytes 49160 | tf_op jit(solution)/shard_map/ppermute | solution.py:22
  44.7 11.4 %collective-permute-start.4 = (bf16[112,512]{1,0:T(8,128)(2,1)S(1)}, bf16[112,512]{1,0:T(8,128)(2,1)S(1)}, u32[]{:S(2)}, u32[]{:S(2)}) collective-permute-start(bf16[112,512]{1,0:T(8,128)(2,1)S(1)} %constant_dynamic-update-slice_fusion.refs_5_.refs_1_), channel_id=1, source_target_pairs={{0,24},{8,0},{16,8},{24,16},{1,25},{9,1},{17,9},{25,17},{2,26},{10... | collective-permute-start | bytes 344072 | tf_op jit(solution)/shard_map/ppermute | solution.py:22
  47.5 8.6 %collective-permute-start.3 = (bf16[112,512]{1,0:T(8,128)(2,1)S(1)}, bf16[112,512]{1,0:T(8,128)(2,1)S(1)}, u32[]{:S(2)}, u32[]{:S(2)}) collective-permute-start(bf16[112,512]{1,0:T(8,128)(2,1)S(1)} %constant_dynamic-update-slice_fusion.refs_5_.refs_1_), channel_id=1, source_target_pairs={{0,8},{8,16},{16,24},{24,0},{1,9},{9,17},{17,25},{25,1},{2,10},{10... | collective-permute-start | bytes 344072 | tf_op jit(solution)/shard_map/ppermute | solution.py:22
  48.2 7.9 %collective-permute-start.5 = (bf16[16,512]{1,0:T(8,128)(2,1)S(1)}, bf16[16,512]{1,0:T(8,128)(2,1)S(1)}, u32[]{:S(2)}, u32[]{:S(2)}) collective-permute-start(bf16[16,512]{1,0:T(8,128)(2,1)S(1)} %reshape_squeeze.7), channel_id=1, source_target_pairs={{0,16},{8,24},{16,0},{24,8},{1,17},{9,25},{17,1},{25,9},{2,18},{10... | collective-permute-start | bytes 49160 | tf_op jit(solution)/shard_map/ppermute | solution.py:22
  74.9 6.9 %collective-permute-start.7 = (bf16[112,512]{1,0:T(8,128)(2,1)S(1)}, bf16[112,512]{1,0:T(8,128)(2,1)S(1)}, u32[]{:S(2)}, u32[]{:S(2)}) collective-permute-start(bf16[112,512]{1,0:T(8,128)(2,1)S(1)} %get-tuple-element.254), channel_id=1, source_target_pairs={{0,8},{8,16},{16,24},{24,0},{1,9},{9,17},{17,25},{25,1},{2,10},{10... | collective-permute-start | bytes 344072 | tf_op jit(solution)/shard_map/ppermute | solution.py:22
  75.8 6.9 %collective-permute-start.10 = (bf16[16,512]{1,0:T(8,128)(2,1)S(1)}, bf16[16,512]{1,0:T(8,128)(2,1)S(1)}, u32[]{:S(2)}, u32[]{:S(2)}) collective-permute-start(bf16[16,512]{1,0:T(8,128)(2,1)S(1)} %slice.449), channel_id=1, source_target_pairs={{0,16},{8,24},{16,0},{24,8},{1,17},{9,25},{17,1},{25,9},{2,18},{10... | collective-permute-start | bytes 49160 | tf_op jit(solution)/shard_map/ppermute | solution.py:22
  83.4 8.0 %all-to-all-start = ((bf16[8,2,512]{2,1,0:T(2,128)(2,1)}), bf16[8,2,512]{2,1,0:T(2,128)(2,1)S(1)}, u32[]{:S(2)}, u32[]{:S(2)}) async-start(bf16[8,2,512]{2,1,0:T(2,128)(2,1)} %reshape.258), calls=%async_computation | async-start | bytes 32768 | tf_op jit(solution)/shard_map/all_to_all | solution.py:421
  108.0 9.6 %collective-permute-start.38 = (f32[2,4,512]{2,1,0:T(4,128)S(1)}, f32[2,4,512]{2,1,0:T(4,128)S(1)}, u32[]{:S(2)}, u32[]{:S(2)}) collective-permute-start(f32[2,4,512]{2,1,0:T(4,128)S(1)} %fusion.17), channel_id=1, source_target_pairs={{0,4},{1,5},{2,6},{3,7},{4,0},{5,1},{6,2},{7,3},{8,12},{9,13},{10,... | collective-permute-start | bytes 49160 | tf_op jit(solution)/shard_map/ppermute | solution.py:27
  117.1 27.8 %collective-permute-start.51 = (bf16[16,7,16,256]{3,2,1,0:T(8,128)(2,1)}, bf16[16,7,16,256]{3,2,1,0:T(8,128)(2,1)}, u32[]{:S(2)}, u32[]{:S(2)}) collective-permute-start(bf16[16,7,16,256]{3,2,1,0:T(8,128)(2,1)} %slice.512), channel_id=1, source_target_pairs={{0,1},{1,0},{2,3},{3,2},{4,5},{5,4},{6,7},{7,6},{8,9},{9,8},{10,11... | collective-permute-start | bytes 2752520 | tf_op jit(solution)/shard_map/ppermute | solution.py:27
  117.1 30.2 %collective-permute-start.41 = (bf16[16,7,16,256]{3,2,1,0:T(8,128)(2,1)S(1)}, bf16[16,7,16,256]{3,2,1,0:T(8,128)(2,1)}, u32[]{:S(2)}, u32[]{:S(2)}) collective-permute-start(bf16[16,7,16,256]{3,2,1,0:T(8,128)(2,1)S(1)} %slice.495), channel_id=1, source_target_pairs={{0,1},{1,0},{2,3},{3,2},{4,5},{5,4},{6,7},{7,6},{8,9},{9,8},{10,11... | collective-permute-start | bytes 2752520 | tf_op jit(solution)/shard_map/ppermute | solution.py:27
  118.5 15.2 %collective-permute-start.11 = (bf16[112,512]{1,0:T(8,128)(2,1)S(1)}, bf16[112,512]{1,0:T(8,128)(2,1)S(1)}, u32[]{:S(2)}, u32[]{:S(2)}) collective-permute-start(bf16[112,512]{1,0:T(8,128)(2,1)S(1)} %get-tuple-element.251), channel_id=1, source_target_pairs={{0,24},{8,0},{16,8},{24,16},{1,25},{9,1},{17,9},{25,17},{2,26},{10... | collective-permute-start | bytes 344072 | tf_op jit(solution)/shard_map/ppermute | solution.py:22
  120.3 13.4 %collective-permute-start.12 = (bf16[112,512]{1,0:T(8,128)(2,1)S(1)}, bf16[112,512]{1,0:T(8,128)(2,1)S(1)}, u32[]{:S(2)}, u32[]{:S(2)}) collective-permute-start(bf16[112,512]{1,0:T(8,128)(2,1)S(1)} %get-tuple-element.252), channel_id=1, source_target_pairs={{0,8},{8,16},{16,24},{24,0},{1,9},{9,17},{17,25},{25,1},{2,10},{10... | collective-permute-start | bytes 344072 | tf_op jit(solution)/shard_map/ppermute | solution.py:22
  121.6 9.5 %collective-permute-start.40 = (f32[2,4,512]{2,1,0:T(4,128)S(1)}, f32[2,4,512]{2,1,0:T(4,128)S(1)}, u32[]{:S(2)}, u32[]{:S(2)}) collective-permute-start(f32[2,4,512]{2,1,0:T(4,128)S(1)} %add.248), channel_id=1, source_target_pairs={{0,16},{8,24},{16,0},{24,8},{1,17},{9,25},{17,1},{25,9},{2,18},{10... | collective-permute-start | bytes 49160 | tf_op jit(solution)/shard_map/ppermute | solution.py:27
  133.7 17.3 %collective-permute-start.26 = (bf16[16,7,16,256]{3,2,1,0:T(8,128)(2,1)}, bf16[16,7,16,256]{3,2,1,0:T(8,128)(2,1)}, u32[]{:S(2)}, u32[]{:S(2)}) collective-permute-start(bf16[16,7,16,256]{3,2,1,0:T(8,128)(2,1)} %slice.478), channel_id=1, source_target_pairs={{0,1},{1,0},{2,3},{3,2},{4,5},{5,4},{6,7},{7,6},{8,9},{9,8},{10,11... | collective-permute-start | bytes 2752520 | tf_op jit(solution)/shard_map/ppermute | solution.py:27
  133.7 19.4 %collective-permute-start.16 = (bf16[16,7,16,256]{3,2,1,0:T(8,128)(2,1)}, bf16[16,7,16,256]{3,2,1,0:T(8,128)(2,1)}, u32[]{:S(2)}, u32[]{:S(2)}) collective-permute-start(bf16[16,7,16,256]{3,2,1,0:T(8,128)(2,1)} %slice.461), channel_id=1, source_target_pairs={{0,1},{1,0},{2,3},{3,2},{4,5},{5,4},{6,7},{7,6},{8,9},{9,8},{10,11... | collective-permute-start | bytes 2752520 | tf_op jit(solution)/shard_map/ppermute | solution.py:27
  136.4 8.4 %all-to-all-start.1 = ((bf16[8,2,512]{2,1,0:T(2,128)(2,1)}), bf16[8,2,512]{2,1,0:T(2,128)(2,1)S(1)}, u32[]{:S(2)}, u32[]{:S(2)}) async-start(bf16[8,2,512]{2,1,0:T(2,128)(2,1)} %reshape.263), calls=%async_computation.1 | async-start | bytes 32768 | tf_op jit(solution)/shard_map/all_to_all | solution.py:421
  144.8 103.5 %collective-permute-start.14 = (bf16[16,512]{1,0:T(8,128)(2,1)S(1)}, bf16[16,512]{1,0:T(8,128)(2,1)S(1)}, u32[]{:S(2)}, u32[]{:S(2)}) collective-permute-start(bf16[16,512]{1,0:T(8,128)(2,1)S(1)} %get-tuple-element.271), channel_id=1, source_target_pairs={{0,1},{1,2},{2,3},{3,4},{4,5},{5,6},{6,7},{7,0},{8,9},{9,10},{10,1... | collective-permute-start | bytes 49160 | tf_op jit(solution)/shard_map/ppermute | solution.py:22
  146.6 13.5 %collective-permute-start.52 = (bf16[8,7,16,256]{3,2,1,0:T(8,128)(2,1)S(1)}, bf16[8,7,16,256]{3,2,1,0:T(8,128)(2,1)S(1)}, u32[]{:S(2)}, u32[]{:S(2)}) collective-permute-start(bf16[8,7,16,256]{3,2,1,0:T(8,128)(2,1)S(1)} %get-tuple-element.216), channel_id=1, source_target_pairs={{0,4},{1,5},{2,6},{3,7},{4,0},{5,1},{6,2},{7,3},{8,12},{9,13},{10,... | collective-permute-start | bytes 1376264 | tf_op jit(solution)/shard_map/ppermute | solution.py:27
  148.7 13.7 %collective-permute-start.42 = (bf16[8,7,16,256]{3,2,1,0:T(8,128)(2,1)S(1)}, bf16[8,7,16,256]{3,2,1,0:T(8,128)(2,1)S(1)}, u32[]{:S(2)}, u32[]{:S(2)}) collective-permute-start(bf16[8,7,16,256]{3,2,1,0:T(8,128)(2,1)S(1)} %get-tuple-element.218), channel_id=1, source_target_pairs={{0,2},{1,3},{2,0},{3,1},{4,6},{5,7},{6,4},{7,5},{8,10},{9,11},{10,... | collective-permute-start | bytes 1376264 | tf_op jit(solution)/shard_map/ppermute | solution.py:27
  152.5 17.4 %collective-permute-start.27 = (bf16[8,7,16,256]{3,2,1,0:T(8,128)(2,1)S(1)}, bf16[8,7,16,256]{3,2,1,0:T(8,128)(2,1)S(1)}, u32[]{:S(2)}, u32[]{:S(2)}) collective-permute-start(bf16[8,7,16,256]{3,2,1,0:T(8,128)(2,1)S(1)} %get-tuple-element.220), channel_id=1, source_target_pairs={{0,4},{1,5},{2,6},{3,7},{4,0},{5,1},{6,2},{7,3},{8,12},{9,13},{10,... | collective-permute-start | bytes 1376264 | tf_op jit(solution)/shard_map/ppermute | solution.py:27
  154.6 17.7 %collective-permute-start.17 = (bf16[8,7,16,256]{3,2,1,0:T(8,128)(2,1)S(1)}, bf16[8,7,16,256]{3,2,1,0:T(8,128)(2,1)S(1)}, u32[]{:S(2)}, u32[]{:S(2)}) collective-permute-start(bf16[8,7,16,256]{3,2,1,0:T(8,128)(2,1)S(1)} %get-tuple-element.222), channel_id=1, source_target_pairs={{0,2},{1,3},{2,0},{3,1},{4,6},{5,7},{6,4},{7,5},{8,10},{9,11},{10,... | collective-permute-start | bytes 1376264 | tf_op jit(solution)/shard_map/ppermute | solution.py:27
  160.2 17.0 %collective-permute-start.53 = (bf16[4,7,16,256]{3,2,1,0:T(8,128)(2,1)S(1)}, bf16[4,7,16,256]{3,2,1,0:T(8,128)(2,1)S(1)}, u32[]{:S(2)}, u32[]{:S(2)}) collective-permute-start(bf16[4,7,16,256]{3,2,1,0:T(8,128)(2,1)S(1)} %get-tuple-element.224), channel_id=1, source_target_pairs={{0,2},{1,3},{2,0},{3,1},{4,6},{5,7},{6,4},{7,5},{8,10},{9,11},{10,... | collective-permute-start | bytes 688136 | tf_op jit(solution)/shard_map/ppermute | solution.py:27
  162.6 17.0 %collective-permute-start.43 = (bf16[4,7,16,256]{3,2,1,0:T(8,128)(2,1)S(1)}, bf16[4,7,16,256]{3,2,1,0:T(8,128)(2,1)S(1)}, u32[]{:S(2)}, u32[]{:S(2)}) collective-permute-start(bf16[4,7,16,256]{3,2,1,0:T(8,128)(2,1)S(1)} %get-tuple-element.226), channel_id=1, source_target_pairs={{0,4},{1,5},{2,6},{3,7},{4,0},{5,1},{6,2},{7,3},{8,12},{9,13},{10,... | collective-permute-start | bytes 688136 | tf_op jit(solution)/shard_map/ppermute | solution.py:27
  170.0 16.5 %collective-permute-start.28 = (bf16[4,7,16,256]{3,2,1,0:T(8,128)(2,1)S(1)}, bf16[4,7,16,256]{3,2,1,0:T(8,128)(2,1)S(1)}, u32[]{:S(2)}, u32[]{:S(2)}) collective-permute-start(bf16[4,7,16,256]{3,2,1,0:T(8,128)(2,1)S(1)} %get-tuple-element.228), channel_id=1, source_target_pairs={{0,2},{1,3},{2,0},{3,1},{4,6},{5,7},{6,4},{7,5},{8,10},{9,11},{10,... | collective-permute-start | bytes 688136 | tf_op jit(solution)/shard_map/ppermute | solution.py:27
  172.4 16.3 %collective-permute-start.18 = (bf16[4,7,16,256]{3,2,1,0:T(8,128)(2,1)S(1)}, bf16[4,7,16,256]{3,2,1,0:T(8,128)(2,1)S(1)}, u32[]{:S(2)}, u32[]{:S(2)}) collective-permute-start(bf16[4,7,16,256]{3,2,1,0:T(8,128)(2,1)S(1)} %get-tuple-element.230), channel_id=1, source_target_pairs={{0,4},{1,5},{2,6},{3,7},{4,0},{5,1},{6,2},{7,3},{8,12},{9,13},{10,... | collective-permute-start | bytes 688136 | tf_op jit(solution)/shard_map/ppermute | solution.py:27
  177.2 6.1 %collective-permute-start.54 = (bf16[2,7,16,256]{3,2,1,0:T(8,128)(2,1)S(1)}, bf16[2,7,16,256]{3,2,1,0:T(8,128)(2,1)S(1)}, u32[]{:S(2)}, u32[]{:S(2)}) collective-permute-start(bf16[2,7,16,256]{3,2,1,0:T(8,128)(2,1)S(1)} %get-tuple-element.234), channel_id=1, source_target_pairs={{0,8},{8,0},{16,24},{24,16},{1,9},{9,1},{17,25},{25,17},{2,10},{10... | collective-permute-start | bytes 344072 | tf_op jit(solution)/shard_map/ppermute | solution.py:27
  183.4 9.5 %collective-permute-start.55 = (bf16[1,7,16,256]{3,2,1,0:T(8,128)(2,1)S(1)}, bf16[1,7,16,256]{3,2,1,0:T(8,128)(2,1)S(1)}, u32[]{:S(2)}, u32[]{:S(2)}) collective-permute-start(bf16[1,7,16,256]{3,2,1,0:T(8,128)(2,1)S(1)} %add_convert_fusion.25), channel_id=1, source_target_pairs={{0,16},{8,24},{16,0},{24,8},{1,17},{9,25},{17,1},{25,9},{2,18},{10... | collective-permute-start | bytes 172040 | tf_op jit(solution)/shard_map/ppermute | solution.py:27
  186.6 17.7 %collective-permute-start.29 = (bf16[2,7,16,256]{3,2,1,0:T(8,128)(2,1)S(1)}, bf16[2,7,16,256]{3,2,1,0:T(8,128)(2,1)S(1)}, u32[]{:S(2)}, u32[]{:S(2)}) collective-permute-start(bf16[2,7,16,256]{3,2,1,0:T(8,128)(2,1)S(1)} %get-tuple-element.242), channel_id=1, source_target_pairs={{0,8},{8,0},{16,24},{24,16},{1,9},{9,1},{17,25},{25,17},{2,10},{10... | collective-permute-start | bytes 344072 | tf_op jit(solution)/shard_map/ppermute | solution.py:27
  188.8 13.6 %collective-permute-start.19 = (bf16[2,7,16,256]{3,2,1,0:T(8,128)(2,1)S(1)}, bf16[2,7,16,256]{3,2,1,0:T(8,128)(2,1)S(1)}, u32[]{:S(2)}, u32[]{:S(2)}) collective-permute-start(bf16[2,7,16,256]{3,2,1,0:T(8,128)(2,1)S(1)} %get-tuple-element.246), channel_id=1, source_target_pairs={{0,8},{8,0},{16,24},{24,16},{1,9},{9,1},{17,25},{25,17},{2,10},{10... | collective-permute-start | bytes 344072 | tf_op jit(solution)/shard_map/ppermute | solution.py:27
  191.5 9.0 %collective-permute-start.46 = (bf16[1,7,16,256]{3,2,1,0:T(8,128)(2,1)S(1)}, bf16[1,7,16,256]{3,2,1,0:T(8,128)(2,1)S(1)}, u32[]{:S(2)}, u32[]{:S(2)}) collective-permute-start(bf16[1,7,16,256]{3,2,1,0:T(8,128)(2,1)S(1)} %get-tuple-element.206), channel_id=1, source_target_pairs={{0,16},{8,24},{16,0},{24,8},{1,17},{9,25},{17,1},{25,9},{2,18},{10... | collective-permute-start | bytes 172040 | tf_op jit(solution)/shard_map/ppermute | solution.py:27
  198.9 15.7 %collective-permute-start.57 = (bf16[2,7,16,256]{3,2,1,0:T(8,128)(2,1)S(1)}, bf16[2,7,16,256]{3,2,1,0:T(8,128)(2,1)S(1)}, u32[]{:S(2)}, u32[]{:S(2)}) collective-permute-start(bf16[2,7,16,256]{3,2,1,0:T(8,128)(2,1)S(1)} %pad_maximum_fusion.12), channel_id=1, source_target_pairs={{0,8},{8,0},{16,24},{24,16},{1,9},{9,1},{17,25},{25,17},{2,10},{10... | collective-permute-start | bytes 344072 | tf_op jit(solution)/shard_map/ppermute | solution.py:27
  200.5 15.0 %collective-permute-start.47 = (bf16[2,7,16,256]{3,2,1,0:T(8,128)(2,1)S(1)}, bf16[2,7,16,256]{3,2,1,0:T(8,128)(2,1)S(1)}, u32[]{:S(2)}, u32[]{:S(2)}) collective-permute-start(bf16[2,7,16,256]{3,2,1,0:T(8,128)(2,1)S(1)} %pad_maximum_fusion.11), channel_id=1, source_target_pairs={{0,8},{8,0},{16,24},{24,16},{1,9},{9,1},{17,25},{25,17},{2,10},{10... | collective-permute-start | bytes 344072 | tf_op jit(solution)/shard_map/ppermute | solution.py:27
  202.4 6.8 %collective-permute-start.20 = (bf16[1,7,16,256]{3,2,1,0:T(8,128)(2,1)S(1)}, bf16[1,7,16,256]{3,2,1,0:T(8,128)(2,1)S(1)}, u32[]{:S(2)}, u32[]{:S(2)}) collective-permute-start(bf16[1,7,16,256]{3,2,1,0:T(8,128)(2,1)S(1)} %add_convert_fusion.34), channel_id=1, source_target_pairs={{0,16},{8,24},{16,0},{24,8},{1,17},{9,25},{17,1},{25,9},{2,18},{10... | collective-permute-start | bytes 172040 | tf_op jit(solution)/shard_map/ppermute | solution.py:27
  209.8 10.7 %collective-permute-start.21 = (bf16[1,7,16,256]{3,2,1,0:T(8,128)(2,1)S(1)}, bf16[1,7,16,256]{3,2,1,0:T(8,128)(2,1)S(1)}, u32[]{:S(2)}, u32[]{:S(2)}) collective-permute-start(bf16[1,7,16,256]{3,2,1,0:T(8,128)(2,1)S(1)} %get-tuple-element.210), channel_id=1, source_target_pairs={{0,16},{8,24},{16,0},{24,8},{1,17},{9,25},{17,1},{25,9},{2,18},{10... | collective-permute-start | bytes 172040 | tf_op jit(solution)/shard_map/ppermute | solution.py:27
  211.4 7.2 %collective-permute-start.31 = (bf16[1,7,16,256]{3,2,1,0:T(8,128)(2,1)S(1)}, bf16[1,7,16,256]{3,2,1,0:T(8,128)(2,1)S(1)}, u32[]{:S(2)}, u32[]{:S(2)}) collective-permute-start(bf16[1,7,16,256]{3,2,1,0:T(8,128)(2,1)S(1)} %get-tuple-element.208), channel_id=1, source_target_pairs={{0,16},{8,24},{16,0},{24,8},{1,17},{9,25},{17,1},{25,9},{2,18},{10... | collective-permute-start | bytes 172040 | tf_op jit(solution)/shard_map/ppermute | solution.py:27
  214.7 13.1 %collective-permute-start.58 = (bf16[4,7,16,256]{3,2,1,0:T(8,128)(2,1)S(1)}, bf16[4,7,16,256]{3,2,1,0:T(8,128)(2,1)S(1)}, u32[]{:S(2)}, u32[]{:S(2)}) collective-permute-start(bf16[4,7,16,256]{3,2,1,0:T(8,128)(2,1)S(1)} %pad_maximum_fusion.7), channel_id=1, source_target_pairs={{0,2},{1,3},{2,0},{3,1},{4,6},{5,7},{6,4},{7,5},{8,10},{9,11},{10,... | collective-permute-start | bytes 688136 | tf_op jit(solution)/shard_map/ppermute | solution.py:27
  215.5 13.5 %collective-permute-start.48 = (bf16[4,7,16,256]{3,2,1,0:T(8,128)(2,1)S(1)}, bf16[4,7,16,256]{3,2,1,0:T(8,128)(2,1)S(1)}, u32[]{:S(2)}, u32[]{:S(2)}) collective-permute-start(bf16[4,7,16,256]{3,2,1,0:T(8,128)(2,1)S(1)} %pad_maximum_fusion.6), channel_id=1, source_target_pairs={{0,4},{1,5},{2,6},{3,7},{4,0},{5,1},{6,2},{7,3},{8,12},{9,13},{10,... | collective-permute-start | bytes 688136 | tf_op jit(solution)/shard_map/ppermute | solution.py:27
  223.5 8.6 %collective-permute-start.33 = (bf16[4,7,16,256]{3,2,1,0:T(8,128)(2,1)S(1)}, bf16[4,7,16,256]{3,2,1,0:T(8,128)(2,1)S(1)}, u32[]{:S(2)}, u32[]{:S(2)}) collective-permute-start(bf16[4,7,16,256]{3,2,1,0:T(8,128)(2,1)S(1)} %pad_maximum_fusion.5), channel_id=1, source_target_pairs={{0,2},{1,3},{2,0},{3,1},{4,6},{5,7},{6,4},{7,5},{8,10},{9,11},{10,... | collective-permute-start | bytes 688136 | tf_op jit(solution)/shard_map/ppermute | solution.py:27
  225.4 8.5 %collective-permute-start.23 = (bf16[4,7,16,256]{3,2,1,0:T(8,128)(2,1)S(1)}, bf16[4,7,16,256]{3,2,1,0:T(8,128)(2,1)S(1)}, u32[]{:S(2)}, u32[]{:S(2)}) collective-permute-start(bf16[4,7,16,256]{3,2,1,0:T(8,128)(2,1)S(1)} %pad_maximum_fusion.4), channel_id=1, source_target_pairs={{0,4},{1,5},{2,6},{3,7},{4,0},{5,1},{6,2},{7,3},{8,12},{9,13},{10,... | collective-permute-start | bytes 688136 | tf_op jit(solution)/shard_map/ppermute | solution.py:27
  227.8 13.9 %collective-permute-start.59 = (bf16[8,7,16,256]{3,2,1,0:T(8,128)(2,1)S(1)}, bf16[8,7,16,256]{3,2,1,0:T(8,128)(2,1)S(1)}, u32[]{:S(2)}, u32[]{:S(2)}) collective-permute-start(bf16[8,7,16,256]{3,2,1,0:T(8,128)(2,1)S(1)} %pad_maximum_fusion.3), channel_id=1, source_target_pairs={{0,4},{1,5},{2,6},{3,7},{4,0},{5,1},{6,2},{7,3},{8,12},{9,13},{10,... | collective-permute-start | bytes 1376264 | tf_op jit(solution)/shard_map/ppermute | solution.py:27
  229.1 11.7 %collective-permute-start.49 = (bf16[8,7,16,256]{3,2,1,0:T(8,128)(2,1)S(1)}, bf16[8,7,16,256]{3,2,1,0:T(8,128)(2,1)S(1)}, u32[]{:S(2)}, u32[]{:S(2)}) collective-permute-start(bf16[8,7,16,256]{3,2,1,0:T(8,128)(2,1)S(1)} %pad_maximum_fusion.2), channel_id=1, source_target_pairs={{0,2},{1,3},{2,0},{3,1},{4,6},{5,7},{6,4},{7,5},{8,10},{9,11},{10,... | collective-permute-start | bytes 1376264 | tf_op jit(solution)/shard_map/ppermute | solution.py:27
  232.1 14.7 %collective-permute-start.34 = (bf16[8,7,16,256]{3,2,1,0:T(8,128)(2,1)S(1)}, bf16[8,7,16,256]{3,2,1,0:T(8,128)(2,1)S(1)}, u32[]{:S(2)}, u32[]{:S(2)}) collective-permute-start(bf16[8,7,16,256]{3,2,1,0:T(8,128)(2,1)S(1)} %pad_maximum_fusion.1), channel_id=1, source_target_pairs={{0,4},{1,5},{2,6},{3,7},{4,0},{5,1},{6,2},{7,3},{8,12},{9,13},{10,... | collective-permute-start | bytes 1376264 | tf_op jit(solution)/shard_map/ppermute | solution.py:27
  234.0 11.7 %collective-permute-start.24 = (bf16[8,7,16,256]{3,2,1,0:T(8,128)(2,1)S(1)}, bf16[8,7,16,256]{3,2,1,0:T(8,128)(2,1)S(1)}, u32[]{:S(2)}, u32[]{:S(2)}) collective-permute-start(bf16[8,7,16,256]{3,2,1,0:T(8,128)(2,1)S(1)} %pad_maximum_fusion), channel_id=1, source_target_pairs={{0,2},{1,3},{2,0},{3,1},{4,6},{5,7},{6,4},{7,5},{8,10},{9,11},{10,... | collective-permute-start | bytes 1376264 | tf_op jit(solution)/shard_map/ppermute | solution.py:27
  241.7 6.7 %collective-permute-start.50 = (bf16[16,7,16,256]{3,2,1,0:T(8,128)(2,1)}, bf16[16,7,16,256]{3,2,1,0:T(8,128)(2,1)S(1)}, u32[]{:S(2)}, u32[]{:S(2)}) collective-permute-start(bf16[16,7,16,256]{3,2,1,0:T(8,128)(2,1)} %get-tuple-element.235), channel_id=1, source_target_pairs={{0,1},{1,0},{2,3},{3,2},{4,5},{5,4},{6,7},{7,6},{8,9},{9,8},{10,11... | collective-permute-start | bytes 2752520 | tf_op jit(solution)/shard_map/ppermute | solution.py:27
  246.8 9.9 %collective-permute-start.25 = (bf16[16,7,16,256]{3,2,1,0:T(8,128)(2,1)}, bf16[16,7,16,256]{3,2,1,0:T(8,128)(2,1)}, u32[]{:S(2)}, u32[]{:S(2)}) collective-permute-start(bf16[16,7,16,256]{3,2,1,0:T(8,128)(2,1)} %get-tuple-element.243), channel_id=1, source_target_pairs={{0,1},{1,0},{2,3},{3,2},{4,5},{5,4},{6,7},{7,6},{8,9},{9,8},{10,11... | collective-permute-start | bytes 2752520 | tf_op jit(solution)/shard_map/ppermute | solution.py:27
  247.8 11.1 %collective-permute-start.35 = (bf16[16,7,16,256]{3,2,1,0:T(8,128)(2,1)}, bf16[16,7,16,256]{3,2,1,0:T(8,128)(2,1)}, u32[]{:S(2)}, u32[]{:S(2)}) collective-permute-start(bf16[16,7,16,256]{3,2,1,0:T(8,128)(2,1)} %get-tuple-element.239), channel_id=1, source_target_pairs={{0,1},{1,0},{2,3},{3,2},{4,5},{5,4},{6,7},{7,6},{8,9},{9,8},{10,11... | collective-permute-start | bytes 2752520 | tf_op jit(solution)/shard_map/ppermute | solution.py:27
  (34 other events, 150.1 us)
